TPU v7x, 32 devices: a whole 2x2x4 slice. The times are simulated.
32 devices in a mesh: groups: 2 (over y), tensor: 16 (over z, x, core).
Axes of the slice: x: 2, y: 2, z: 4, core: 2. Of those that a mesh axis runs over, the one named last changes fastest.
Arguments:
- tokens: bfloat16 [64, 8192], P(('groups', 'tensor')), parts along dimension 0, may hold values from -6 to 6
- out_grad: bfloat16 [64, 8192], P(('groups', 'tensor')), parts along dimension 0, may hold values from -6 to 6
- w_gate: bfloat16 [8192, 16384], P(None, 'tensor'), may hold values from -0.0625 to 0.0625
- w_up: bfloat16 [8192, 16384], P(None, 'tensor'), may hold values from -0.0625 to 0.0625
- w_down: bfloat16 [16384, 8192], P('tensor'), may hold values from -0.046875 to 0.046875
- deltas: bfloat16 [6, 64, 128, 128], P('groups', 'tensor'), parts along dimension 0, may hold values from -0.1875 to 0.1875
- model_block: int32 [6, 64], P('groups', 'tensor'), parts along dimension 0, may hold values from 0 to 63
- hidden_block: int32 [6, 64], P('groups', 'tensor'), parts along dimension 0, may hold values from 0 to 127, as said below
- live_count: int32 [6, 16], P('groups', 'tensor'), parts along dimension 0, may hold values from 1 to 4
- prior_mean: float32 [6, 64, 128, 128], P('groups', 'tensor'), parts along dimension 0, may hold values from -6 to 6
- prior_square: float32 [6, 64, 128, 128], P('groups', 'tensor'), parts along dimension 0, may hold values from 0.01 to 1
Outputs:
- input_grad: bfloat16 [64, 8192], P(('groups', 'tensor')), parts along dimension 0
- moment_mean: float32 [6, 64, 128, 128], P('groups', 'tensor'), parts along dimension 0
- moment_square: float32 [6, 64, 128, 128], P('groups', 'tensor'), parts along dimension 0
There are 2 independent parts, one for each index of `groups`. A program takes and returns all parts, laid end to end along the dimension named above; an argument that names none is the same for every part. Nothing has to cross between parts.
Inputs may be any that keep to these rules, and one draw needn't show every extreme that they name: `hidden_block`: the slots s of index j of tensor (j * 4 <= s < (j + 1) * 4) lie in hidden blocks j * 8 to (j + 1) * 8 - 1.
All inputs are finite; a program needn't handle non-finite values.
Results may differ from a plain program's by a relative error of at most 0.005.
Values may be sent and summed in bfloat16 or wider, within the bound.
No kernel may reach another device: no remote copies, remote signals or barrier semaphores. Data moves between devices by JAX's collectives and lax.ppermute only.
A program may use at most 128 MiB of HBM per device.

v0:
```python
import jax
import jax.numpy as jnp
from jax import lax
from jax.sharding import PartitionSpec as P

BS = 128


def pick(values, index):
    count = values.shape[0]
    return jnp.take(values.reshape(count, -1, BS), index, axis=1)


def spread(contrib, table):
    placed = jnp.einsum("psj,sc->pcj", contrib, table, precision=lax.Precision.HIGHEST)
    return placed.reshape(contrib.shape[0], -1)


def activate(gate_pre, up_pre, grad_act):
    sigma = jax.nn.sigmoid(gate_pre)
    silu_gate = gate_pre * sigma
    activ = (silu_gate * up_pre).astype(jnp.bfloat16)
    grad_up = (grad_act * silu_gate).astype(jnp.bfloat16)
    grad_gate = (grad_act * up_pre * sigma * (1.0 + gate_pre * (1.0 - sigma))).astype(jnp.bfloat16)
    return (activ, grad_up, grad_gate)


def per_device(
    tokens,
    out_grad,
    w_gate,
    w_up,
    w_down,
    deltas,
    model_block,
    hidden_block,
    live_count,
    prior_mean,
    prior_square,
):
    slots = deltas.shape[1]
    hidden_cols = w_gate.shape[1] // BS
    model_cols = w_gate.shape[0] // BS
    live = jnp.arange(slots)[None, :] < live_count
    active = jnp.where(live[:, :, None, None], deltas, jnp.zeros_like(deltas))
    local_hidden = hidden_block - lax.axis_index("tensor") * hidden_cols
    hidden_table = (local_hidden[:, :, None] == jnp.arange(hidden_cols)[None, None, :]).astype(
        jnp.float32
    )
    model_table = (model_block[:, :, None] == jnp.arange(model_cols)[None, None, :]).astype(
        jnp.float32
    )
    contract = (((1,), (1,)), ((), ()))
    rows_x = lax.all_gather(tokens, "tensor", axis=0, tiled=True)
    picked_gate = pick(rows_x, model_block[0])
    picked_up = pick(rows_x, model_block[1])
    gate_pre = jnp.dot(rows_x, w_gate, preferred_element_type=jnp.float32) + spread(
        jnp.einsum("psk,skj->psj", picked_gate, active[0], preferred_element_type=jnp.float32),
        hidden_table[0],
    )
    up_pre = jnp.dot(rows_x, w_up, preferred_element_type=jnp.float32) + spread(
        jnp.einsum("psk,skj->psj", picked_up, active[1], preferred_element_type=jnp.float32),
        hidden_table[1],
    )
    gate_pre, up_pre, picked_gate, picked_up = (gate_pre, up_pre, picked_gate, picked_up)
    rows_dy = lax.all_gather(out_grad, "tensor", axis=0, tiled=True)
    picked_down = pick(rows_dy, model_block[2])
    grad_act = lax.dot_general(
        rows_dy, w_down, contract, preferred_element_type=jnp.float32
    ) + spread(
        jnp.einsum("psk,sjk->psj", picked_down, active[2], preferred_element_type=jnp.float32),
        hidden_table[2],
    )
    grad_act, picked_down = (grad_act, picked_down)
    activ, grad_up, grad_gate = activate(gate_pre, up_pre, grad_act)
    block_gate = jnp.einsum(
        "tsk,tsj->skj",
        picked_gate,
        pick(grad_gate, local_hidden[0]),
        preferred_element_type=jnp.float32,
    )
    block_up = jnp.einsum(
        "tsk,tsj->skj",
        picked_up,
        pick(grad_up, local_hidden[1]),
        preferred_element_type=jnp.float32,
    )
    block_down = jnp.einsum(
        "tsk,tsj->skj",
        pick(activ, local_hidden[2]),
        picked_down,
        preferred_element_type=jnp.float32,
    )
    grads = jnp.stack([block_gate, block_up, block_down])
    dense = lax.dot_general(grad_gate, w_gate, contract, preferred_element_type=jnp.float32)
    dense = dense + lax.dot_general(grad_up, w_up, contract, preferred_element_type=jnp.float32)
    back_gate = jnp.einsum(
        "psj,skj->psk",
        pick(grad_gate, local_hidden[0]),
        active[0],
        preferred_element_type=jnp.float32,
    )
    back_up = jnp.einsum(
        "psj,skj->psk",
        pick(grad_up, local_hidden[1]),
        active[1],
        preferred_element_type=jnp.float32,
    )
    input_grad = lax.psum_scatter(
        dense + spread(back_gate, model_table[0]) + spread(back_up, model_table[1]),
        "tensor",
        scatter_dimension=0,
        tiled=True,
    ).astype(jnp.bfloat16)
    keep = live[:, :, None, None]
    moment_mean = jnp.where(keep, 0.9 * prior_mean + 0.1 * grads, prior_mean)
    moment_square = jnp.where(keep, 0.999 * prior_square + 0.001 * grads * grads, prior_square)
    return (input_grad, moment_mean, moment_square)


def solution(mesh):
    placed = (
        P(("groups", "tensor"), None),
        P(("groups", "tensor"), None),
        P(None, "tensor"),
        P(None, "tensor"),
        P("tensor", None),
        P("groups", "tensor", None, None),
        P("groups", "tensor"),
        P("groups", "tensor"),
        P("groups", "tensor"),
        P("groups", "tensor", None, None),
        P("groups", "tensor", None, None),
    )
    return jax.shard_map(
        per_device,
        mesh=mesh,
        in_specs=placed,
        out_specs=(
            P(("groups", "tensor"), None),
            P("groups", "tensor", None, None),
            P("groups", "tensor", None, None),
        ),
        check_vma=False,
    )
```

profile of v0, /device:TPU:0, one launch (start us, length us, event | category | flops | bytes accessed | tf_op | source)
XLA Modules:
  0.0 185.5 jit_solution(5496128284119757869)
XLA Ops:
  0.6 24.8 %all-gather.1 = bf16[16,2,8192]{2,1,0:T(2,128)(2,1)S(1)} all-gather(bf16[1,2,8192]{2,1,0:T(2,128)(2,1)} %bitcast.150), channel_id=1, replica_groups=mesh['groups'=2,'tensor'=16] {'tensor'}, dimensions={0}, use_global_device_ids=true | all-gather | bytes 557056 | tf_op jit(solution)/shard_map/all_gather | solution.py:54
  25.5 0.2 reshape.140
  25.7 0.7 iota_compare_fusion.2
  26.4 1.1 broadcast_select_fusion
  27.5 0.4 reshape.75
  27.9 0.3 copy.30
  28.2 0.8 compare_and_fusion.4
  29.1 0.6 gather_fusion.1
  29.6 0.2 convolution_bitcast_fusion.4
  29.8 0.7 broadcast_subtract_fusion
  30.5 0.1 iota_compare_fusion.1
  30.6 0.3 fusion.12
  30.8 8.7 %convolution_add_fusion.2 = f32[32,1024]{1,0:T(8,128)S(1)} fusion(bf16[32,8192]{1,0:T(8,128)(2,1)S(1)} %reshape.140, bf16[8192,1024]{1,0:T(8,128)(2,1)} %param.18, f32[4,8,8,128]{3,2,1,0:T(8,128)S(1)} %bitcast.148), kind=kOutput, calls=%fused_computation.14 | convolution fusion | flops 536903680 | bytes 17563648 | tf_op jit(solution)/shard_map/dot_general | solution.py:61
  39.6 0.0 copy-start
  39.6 0.6 gather_fusion.2
  40.2 0.2 convolution_bitcast_fusion.3
  40.4 0.3 fusion.10
  40.6 8.8 %convolution_add_fusion.1 = f32[32,1024]{1,0:T(8,128)S(1)} fusion(bf16[32,8192]{1,0:T(8,128)(2,1)S(1)} %reshape.140, bf16[8192,1024]{1,0:T(8,128)(2,1)} %param.17, f32[4,8,8,128]{3,2,1,0:T(8,128)S(1)} %bitcast.147), kind=kOutput, calls=%fused_computation.13 | convolution fusion | flops 536903680 | bytes 17563648 | tf_op jit(solution)/shard_map/dot_general | solution.py:57
  49.4 0.0 copy-done
  49.4 19.1 %all-gather = bf16[16,2,8192]{2,1,0:T(2,128)(2,1)S(1)} all-gather(bf16[1,2,8192]{2,1,0:T(2,128)(2,1)S(1)} %bitcast.151), channel_id=1, replica_groups=mesh['groups'=2,'tensor'=16] {'tensor'}, dimensions={0}, use_global_device_ids=true | all-gather | bytes 557056 | tf_op jit(solution)/shard_map/all_gather | solution.py:66
  68.5 0.4 reshape.73
  68.9 0.3 copy.28
  69.2 0.6 gather_fusion
  69.8 0.2 convolution_bitcast_fusion.7
  70.0 0.3 fusion.14
  70.3 0.2 reshape.138
  70.5 0.0 copy-start.1
  70.5 10.9 %fusion.5 = (bf16[4,8,8,128]{3,2,1,0:T(8,128)(2,1)S(1)}, bf16[32,1024]{1,0:T(8,128)(2,1)S(1)}, bf16[32,1024]{1,0:T(8,128)(2,1)S(1)}) fusion(f32[32,1024]{1,0:T(8,128)S(1)} %convolution_add_fusion.2, f32[32,1024]{1,0:T(8,128)S(1)} %convolution_add_fusion.1, f32[4,8,8,128]{3,2,1,0:T(8,128)S(1)} %bitcast.146, bf16[32,8192]{1,0:T(8,128)(2,1)S(1)} %reshape.138, ...), kind=kOutput, calls=%fused_computation.34 | convolution fusion | flops 537395200 | bytes 17891328 | tf_op jit(solution)/shard_map/dot_general | solution.py:68
  81.4 10.8 %fusion.38 = f32[32,8192]{1,0:T(8,128)S(1)} fusion(bf16[32,1024]{1,0:T(8,128)(2,1)S(1)} %get-tuple-element.20, bf16[8192,1024]{1,0:T(8,128)(2,1)} %param.17), kind=kOutput, calls=%fused_computation.103 | convolution fusion | flops 536870912 | bytes 17891328 | tf_op jit(solution)/shard_map/dot_general | solution.py:95
  92.2 0.6 gather_fusion.4
  92.8 0.2 convolution_bitcast_fusion.5
  93.0 0.0 copy-done.1
  93.0 0.1 iota_compare_fusion
  93.1 0.6 fusion.6
  93.7 0.6 gather_fusion.3
  94.3 0.2 convolution_bitcast_fusion.6
  94.5 0.6 fusion.8
  95.2 0.0 copy-start.2
  95.2 12.7 %fusion.1 = f32[32,8192]{1,0:T(8,128)} fusion(f32[32,8192]{1,0:T(8,128)S(1)} %fusion.38, bf16[32,1024]{1,0:T(8,128)(2,1)S(1)} %get-tuple-element.21, bf16[8192,1024]{1,0:T(8,128)(2,1)} %param.18, f32[4,8,64,128]{3,2,1,0:T(8,128)S(1)} %bitcast.144, f32[4,8,64,128]{3,2,1,0:T(8,128)S(1)} %bitcast.145), kind=kOutput, calls=%fused_computation.8 | convolution fusion | flops 537657344 | bytes 21037056 | tf_op jit(solution)/shard_map/dot_general | solution.py:96
  107.8 71.3 %all-reduce.2 = bf16[32,8192]{1,0:T(8,128)(2,1)S(1)} all-reduce(f32[32,8192]{1,0:T(8,128)} %fusion.1), channel_id=2, replica_groups=mesh['groups'=2,'tensor'=16] {'tensor'}, use_global_device_ids=true, to_apply=%region_0.0.clone | all-reduce | flops 262144 | bytes 1572864
  179.2 0.0 copy-done.2
  179.2 0.6 dynamic-slice
  180.4 0.7 dynamic-slice_convert_fusion
  181.1 0.6 gather_fusion.5
  181.7 0.3 convolution_bitcast_fusion
  182.0 0.3 convolution_bitcast_fusion.1
  182.3 0.3 convolution_bitcast_fusion.2
  182.6 2.9 %fusion.3 = (f32[3,4,128,128]{3,2,1,0:T(8,128)}, f32[3,4,128,128]{3,2,1,0:T(8,128)}) fusion(f32[3,4,128,128]{3,2,1,0:T(8,128)} %param.25, f32[1,4,128,128]{3,2,1,0:T(8,128)S(1)} %convolution_bitcast_fusion, f32[1,4,128,128]{3,2,1,0:T(8,128)S(1)} %convolution_bitcast_fusion.1, f32[1,4,128,128]{3,2,1,0:T(8,128)S(1)} %convolution_bitcast_fusion.2, ...), kind=kLoop, calls=%fused_computation.22 | loop fusion | flops 2162688 | bytes 3932172 | tf_op jit(solution)/shard_map/jit(_where)/select_n | solution.py:117
  (8 shorter events, 0.1 us)
Async XLA Ops:
  39.6 9.8 %copy-start = (bf16[2,8192]{1,0:T(2,128)(2,1)S(1)}, bf16[2,8192]{1,0:T(2,128)(2,1)}, u32[]{:S(2)}) copy-start(bf16[2,8192]{1,0:T(2,128)(2,1)} %param.16) | copy-start | bytes 98308
  70.5 22.5 %copy-start.1 = (s32[3,4]{1,0:T(4,128)S(1)}, s32[3,4]{1,0:T(4,128)}, u32[]{:S(2)}) copy-start(s32[3,4]{1,0:T(4,128)} %param.21) | copy-start | bytes 148
  95.2 84.0 %copy-start.2 = (u32[32]{0:T(128)S(1)}, u32[32]{0:T(128)}, u32[]{:S(2)}) copy-start(u32[32]{0:T(128)} %constant.48) | copy-start | bytes 388
where the time goes:
time: 186 us; the launch traced here: 185 us
  blocking collectives  115 us (62%)
  matrix products  55.8 us (30%)
  local copies, waits for them, and re-layouts  6.55 us (4%)
  other arithmetic  6.37 us (3%)
    unnamed x1, blocking collectives  71.3 us
    all_gather x1, blocking collectives, per_device(): rows_x = lax.all_gather(tokens, 'tensor', axis=0, tiled=True)  24.8 us
    all_gather x1, blocking collectives, per_device(): rows_dy = lax.all_gather(out_grad, 'tensor', axis=0, tiled=True)  19.1 us
    dot_general x1, matrix products, per_device(): lax.dot_general(grad_up, w_up, contract, preferred_element_type=jnp.float32)  12.7 us
    dot_general x1, matrix products, per_device(): lax.dot_general(rows_dy, w_down, contract, preferred_element_type=jnp.flo...  10.9 us
    dot_general x1, matrix products, per_device(): lax.dot_general(grad_gate, w_gate, contract, preferred_element_type=jnp.f...  10.8 us
    dot_general x1, matrix products, per_device(): jnp.dot(rows_x, w_gate, preferred_element_type=jnp.float32)  8.75 us
    dot_general x1, matrix products, per_device(): jnp.dot(rows_x, w_up, preferred_element_type=jnp.float32)  8.75 us

commit v1 on v0

v1 whole, which is shorter than its diff:
```python
import functools

import jax
import jax.numpy as jnp
from jax import lax
from jax.experimental import pallas as pl
from jax.experimental.pallas import tpu as pltpu
from jax.sharding import PartitionSpec as P

BS = 128
MIB = 1 << 20
ROW_BY_ROW = (((1,), (1,)), ((), ()))
BY_TOKEN = (((0,), (0,)), ((), ()))
VMEM = pl.BlockSpec(memory_space=pltpu.VMEM)
SMEM = pl.BlockSpec(memory_space=pltpu.SMEM)
HBM = pl.BlockSpec(memory_space=pltpu.HBM)


def dot(a, b, dims=(((1,), (0,)), ((), ()))):
    return lax.dot_general(a, b, dims, preferred_element_type=jnp.float32)


def load_kernel(start, chunks, w_hbm, out_ref, sem):
    rows = out_ref.shape[0] // chunks
    copies = [
        pltpu.make_async_copy(
            w_hbm.at[pl.ds(start + i * rows, rows)],
            out_ref.at[pl.ds(i * rows, rows)],
            sem.at[i],
        )
        for i in range(chunks)
    ]
    for copy in copies:
        copy.start()
    for copy in copies:
        copy.wait()


def in_hbm(value):
    return pltpu.with_memory_space_constraint(value, pltpu.HBM)


def load(weight, start, rows):
    chunks = 4
    return pl.pallas_call(
        functools.partial(load_kernel, start, chunks),
        out_shape=pltpu.VMEM((rows, weight.shape[1]), weight.dtype),
        in_specs=[HBM],
        out_specs=VMEM,
        scratch_shapes=[pltpu.SemaphoreType.DMA((chunks,))],
        compiler_params=pltpu.CompilerParams(vmem_limit_bytes=MIB),
    )(in_hbm(weight))


def forward_kernel(
    width, mine, theirs, g_lo, g_hi, u_lo, u_hi, w_down, deltas, model, hidden, live,
    rows_ref, activ_ref, up_ref, gate_ref, gate_acc, up_acc, act_acc, d_buf, sem,
):
    half = mine.shape[0]
    slots = deltas.shape[1]
    blocks = gate_ref.shape[1] // BS
    step = w_down.shape[0] // sem.shape[0]
    copies = [
        pltpu.make_async_copy(
            w_down.at[pl.ds(i * step, step)], d_buf.at[pl.ds(i * step, step)], sem.at[i]
        )
        for i in range(sem.shape[0])
    ]
    for copy in copies:
        copy.start()
    rows_ref[0:half, :] = mine[...]
    rows_ref[half : 2 * half, :] = theirs[...]
    depth = g_lo.shape[0]
    gate_acc[...] = dot(rows_ref[:, 0:depth], g_lo[...])
    gate_acc[...] += dot(rows_ref[:, depth:width], g_hi[...])
    up_acc[...] = dot(rows_ref[:, 0:depth], u_lo[...])
    up_acc[...] += dot(rows_ref[:, depth:width], u_hi[...])
    for copy in copies:
        copy.wait()
    act_acc[...] = dot(d_buf[...], rows_ref[:, width:], ROW_BY_ROW)
    grad_act = act_acc[...].T
    for m, acc in ((0, gate_acc), (1, up_acc)):
        for s in range(slots):

            @pl.when(s < live[m])
            def _(m=m, s=s, acc=acc):
                at_m = pl.ds(pl.multiple_of(model[m, s] * BS, BS), BS)
                at_h = pl.ds(pl.multiple_of(lax.rem(hidden[m, s], blocks) * BS, BS), BS)
                acc[:, at_h] += dot(rows_ref[:, at_m], deltas[m, s])

    gate_pre = gate_acc[...]
    up_pre = up_acc[...]
    gate_acc[...] = grad_act
    for s in range(slots):

        @pl.when(s < live[2])
        def _(s=s):
            at_m = pl.ds(pl.multiple_of(width + model[2, s] * BS, BS), BS)
            at_h = pl.ds(pl.multiple_of(lax.rem(hidden[2, s], blocks) * BS, BS), BS)
            gate_acc[:, at_h] += dot(rows_ref[:, at_m], deltas[2, s], ROW_BY_ROW)

    grad_act = gate_acc[...]
    sigma = jax.nn.sigmoid(gate_pre)
    silu_gate = gate_pre * sigma
    activ_ref[...] = (silu_gate * up_pre).astype(jnp.bfloat16)
    up_ref[...] = (grad_act * silu_gate).astype(jnp.bfloat16)
    gate_ref[...] = (grad_act * up_pre * sigma * (1.0 + gate_pre * (1.0 - sigma))).astype(
        jnp.bfloat16
    )


def backward_kernel(
    start, grad_gate, grad_up, g_part, u_part, deltas, model, hidden, live, keep_ref, send_ref, acc
):
    slots = deltas.shape[1]
    blocks = grad_gate.shape[1] // BS
    columns = g_part.shape[0]
    half = keep_ref.shape[0]
    total = dot(g_part[...], grad_gate[...], ROW_BY_ROW)
    total += dot(u_part[...], grad_up[...], ROW_BY_ROW)
    acc[...] = total.T
    for m, grad in ((0, grad_gate), (1, grad_up)):
        for s in range(slots):
            column = model[m, s] * BS - start

            @pl.when((s < live[m]) & (column >= 0) & (column < columns))
            def _(m=m, s=s, grad=grad, column=column):
                at_m = pl.ds(pl.multiple_of(column, BS), BS)
                at_h = pl.ds(pl.multiple_of(lax.rem(hidden[m, s], blocks) * BS, BS), BS)
                acc[:, at_m] += dot(grad[:, at_h], deltas[m, s], ROW_BY_ROW)

    keep_ref[...] = acc[0:half, :]
    send_ref[...] = acc[half:, :].astype(jnp.bfloat16)


def moments_kernel(
    width, rows, activ, grad_up, grad_gate, model, hidden, live, mean, square, mean_out, square_out
):
    slots = mean.shape[1]
    blocks = activ.shape[1] // BS
    for m, grad in ((0, grad_gate), (1, grad_up), (2, activ)):

        @pl.when(pl.program_id(0) == m)
        def _(m=m, grad=grad):
            for s in range(slots):
                at_h = pl.ds(pl.multiple_of(lax.rem(hidden[m, s], blocks) * BS, BS), BS)
                first = width if m == 2 else 0
                at_m = pl.ds(pl.multiple_of(first + model[m, s] * BS, BS), BS)
                if m == 2:
                    block = dot(grad[:, at_h], rows[:, at_m], BY_TOKEN)
                else:
                    block = dot(rows[:, at_m], grad[:, at_h], BY_TOKEN)
                keep = s < live[m]
                old_mean, old_square = mean[0, s], square[0, s]
                mean_out[0, s] = jnp.where(keep, 0.9 * old_mean + 0.1 * block, old_mean)
                square_out[0, s] = jnp.where(
                    keep, 0.999 * old_square + 0.001 * block * block, old_square
                )


def per_device(
    devices,
    tokens,
    out_grad,
    w_gate,
    w_up,
    w_down,
    deltas,
    model_block,
    hidden_block,
    live_count,
    prior_mean,
    prior_square,
):
    width, wide = w_gate.shape
    bits = [1 << k for k in range(devices.bit_length() - 1)]
    count = tokens.shape[0] * devices
    half = count // 2
    part = width // 2
    f32, bf16 = jnp.float32, jnp.bfloat16

    def swap(value, bit):
        return lax.ppermute(value, "tensor", [(i, i ^ bit) for i in range(devices)])

    live = live_count.reshape(-1)
    positions = (model_block, hidden_block, live)
    held = jnp.concatenate([tokens, out_grad], axis=1)
    for bit in bits[:0:-1]:
        came = swap(held, bit)
        held = jnp.concatenate([held, came], axis=0)
    other = swap(held, bits[0])
    g_parts = [load(w_gate, i * part, part) for i in range(2)]
    u_parts = [load(w_up, i * part, part) for i in range(2)]

    rows, activ, grad_up, grad_gate = pl.pallas_call(
        functools.partial(forward_kernel, width),
        out_shape=(
            jax.ShapeDtypeStruct((count, 2 * width), bf16),
            jax.ShapeDtypeStruct((count, wide), bf16),
            jax.ShapeDtypeStruct((count, wide), bf16),
            jax.ShapeDtypeStruct((count, wide), bf16),
        ),
        in_specs=[VMEM] * 6 + [HBM, VMEM] + [SMEM] * 3,
        out_specs=[VMEM] * 4,
        scratch_shapes=[
            pltpu.VMEM((count, wide), f32),
            pltpu.VMEM((count, wide), f32),
            pltpu.VMEM((wide, count), f32),
            pltpu.VMEM((wide, width), bf16),
            pltpu.SemaphoreType.DMA((4,)),
        ],
        compiler_params=pltpu.CompilerParams(vmem_limit_bytes=19 * MIB),
        name="forward",
    )(held, other, *g_parts, *u_parts, in_hbm(w_down), deltas, *positions)

    pieces = []
    for i in range(2):
        keep, send = pl.pallas_call(
            functools.partial(backward_kernel, i * part),
            out_shape=(
                jax.ShapeDtypeStruct((half, part), f32),
                jax.ShapeDtypeStruct((half, part), bf16),
            ),
            in_specs=[VMEM] * 5 + [SMEM] * 3,
            out_specs=[VMEM] * 2,
            scratch_shapes=[pltpu.VMEM((count, part), f32)],
            compiler_params=pltpu.CompilerParams(vmem_limit_bytes=8 * MIB),
        )(grad_gate, grad_up, g_parts[i], u_parts[i], deltas, *positions)
        left = half
        for bit in bits[:-1]:
            total = keep + swap(send, bit).astype(f32)
            left //= 2
            keep, send = total[:left], total[left:].astype(bf16)
        pieces.append((keep + swap(send, bits[-1]).astype(f32)).astype(bf16))
    input_grad = jnp.concatenate(pieces, axis=1)

    slots = deltas.shape[1]
    block = pl.BlockSpec((1, slots, BS, BS), lambda m: (m, 0, 0, 0))
    mean, square = pl.pallas_call(
        functools.partial(moments_kernel, width),
        grid=(3,),
        out_shape=(
            jax.ShapeDtypeStruct(prior_mean.shape, f32),
            jax.ShapeDtypeStruct(prior_square.shape, f32),
        ),
        in_specs=[VMEM] * 4 + [SMEM] * 3 + [block] * 2,
        out_specs=[block] * 2,
        compiler_params=pltpu.CompilerParams(vmem_limit_bytes=8 * MIB),
        name="moments",
    )(rows, activ, grad_up, grad_gate, *positions, prior_mean, prior_square)
    return input_grad, mean, square


def solution(mesh):
    placed = (
        P(("groups", "tensor"), None),
        P(("groups", "tensor"), None),
        P(None, "tensor"),
        P(None, "tensor"),
        P("tensor", None),
        P("groups", "tensor", None, None),
        P("groups", "tensor"),
        P("groups", "tensor"),
        P("groups", "tensor"),
        P("groups", "tensor", None, None),
        P("groups", "tensor", None, None),
    )
    devices = mesh.shape["tensor"]
    return jax.shard_map(
        functools.partial(per_device, devices),
        mesh=mesh,
        in_specs=placed,
        out_specs=(
            P(("groups", "tensor"), None),
            P("groups", "tensor", None, None),
            P("groups", "tensor", None, None),
        ),
        check_vma=False,
    )
```

time: 186 us -> 88.4 us (0.48)
  blocking collectives: 115 us -> 0 us
  matrix products: 55.8 us -> 0 us
  Pallas kernels: 0 us -> 46.5 us
  waiting for transfers between devices: 0 us -> 21.5 us
  starting transfers between devices: 0 us -> 16 us
  other arithmetic: 6.37 us -> 1.5 us
  local copies, waits for them, and re-layouts: 6.55 us -> 1.71 us
    unnamed x1 -> x0, blocking collectives: 71.3 us -> none
    dot_general x18 -> x0, matrix products: 55.8 us -> none  [the longest x1 12.7 us: per_device(): lax.dot_general(grad_up, w_up, contract, preferred_element_type=jnp.float32)]
    pallas_call x0 -> x8, Pallas kernels: none -> 46.5 us  [the longest x1 18.2 us: per_device(): pl.pallas_call(functools.partial(forward_kernel, width), out_shape=(jax.S...]
    all_gather x2 -> x0, blocking collectives: 43.9 us -> none  [the longest x1 24.8 us: per_device(): rows_x = lax.all_gather(tokens, 'tensor', axis=0, tiled=True)]
    ppermute x0 -> x12, waiting for transfers between devices: none -> 21.5 us  [swap(): return lax.ppermute(value, 'tensor', [(i, i ^ bit) for i in range(devices)])]
    ppermute x0 -> x12, starting transfers between devices: none -> 16 us  [swap(): return lax.ppermute(value, 'tensor', [(i, i ^ bit) for i in range(devices)])]
    select_n x2 -> x0, other arithmetic: 3.94 us -> none  [the longest x1 2.85 us: per_device(): jnp.where(keep, 0.999 * prior_square + 0.001 * grads * grads, prior_square)]
    gather x6 -> x0, local copies, waits for them, and re-layouts: 3.36 us -> none  [pick(): return jnp.take(values.reshape(count, -1, BS), index, axis=1)]
  transfers between devices with their start and end apart: 0 -> 12, of which waited for: 0 -> 8; matrix products, arithmetic and copies ran while one was open for 0% -> 0% of each run, Pallas kernels for 0% -> 26%
where the time goes in v1:
time: 88.4 us; the launch traced here: 88.1 us
  Pallas kernels  46.5 us (53%)
  waiting for transfers between devices  21.5 us (24%)
  starting transfers between devices  16 us (18%)
  local copies, waits for them, and re-layouts  1.71 us (2%)
  other arithmetic  1.5 us (2%)
  between operations  0.9 us (1%)
    ppermute x12, waiting for transfers between devices, swap(): return lax.ppermute(value, 'tensor', [(i, i ^ bit) for i in range(devices)])  21.5 us
    pallas_call x1, Pallas kernels, per_device(): pl.pallas_call(functools.partial(forward_kernel, width), out_shape=(jax.S...  18.2 us
    ppermute x12, starting transfers between devices, swap(): return lax.ppermute(value, 'tensor', [(i, i ^ bit) for i in range(devices)])  16 us
    pallas_call x4, Pallas kernels, load(): pl.pallas_call(functools.partial(load_kernel, start, chunks), out_shape=p...  14.1 us
    pallas_call x2, Pallas kernels, per_device(): pl.pallas_call(functools.partial(backward_kernel, i * part), out_shape=(j...  11.4 us
    pallas_call x1, Pallas kernels, per_device(): pl.pallas_call(functools.partial(moments_kernel, width), grid=(3,), out_s...  2.81 us
  transfers between devices with their start and end apart: 12, of which 8 were waited for; matrix products, arithmetic and copies ran while one was open for 0% of the time, Pallas kernels for 26%

profile of v1, /device:TPU:0, one launch (start us, length us, event | category | flops | bytes accessed | tf_op | source)
XLA Modules:
  0.0 88.1 jit_solution(11022330642983555185)
XLA Ops:
  0.6 0.8 constant_dynamic-update-slice_fusion.1
  1.4 0.8 constant_dynamic-update-slice_fusion
  2.2 4.1 %collective-permute-start = (bf16[2,16384]{1,0:T(2,128)(2,1)S(1)}, bf16[2,16384]{1,0:T(2,128)(2,1)S(1)}, u32[]{:S(2)}, u32[]{:S(2)}) collective-permute-start(bf16[2,16384]{1,0:T(2,128)(2,1)S(1)} %constant_dynamic-update-slice_fusion), channel_id=1, source_target_pairs={{0,8},{1,9},{2,10},{3,11},{4,12},{5,13},{6,14},{7,15},{8,0},{9,1},... | collective-permute-start | bytes 196616 | tf_op jit(solution)/shard_map/ppermute | solution.py:183
  6.3 3.6 %collective-permute-done = bf16[2,16384]{1,0:T(2,128)(2,1)S(1)} collective-permute-done((bf16[2,16384]{1,0:T(2,128)(2,1)S(1)}, bf16[2,16384]{1,0:T(2,128)(2,1)S(1)}, u32[]{:S(2)}, u32[]{:S(2)}) %collective-permute-start) | collective-permute-done | bytes 65568 | tf_op jit(solution)/shard_map/ppermute | solution.py:183
  10.0 0.1 pad_maximum_fusion.2
  10.1 0.6 collective-permute-start.1
  10.8 4.4 %collective-permute-done.1 = bf16[4,16384]{1,0:T(4,128)(2,1)S(1)} collective-permute-done((bf16[4,16384]{1,0:T(4,128)(2,1)S(1)}, bf16[4,16384]{1,0:T(4,128)(2,1)S(1)}, u32[]{:S(2)}, u32[]{:S(2)}) %collective-permute-start.1) | collective-permute-done | bytes 131104 | tf_op jit(solution)/shard_map/ppermute | solution.py:183
  15.2 0.2 pad_maximum_fusion.1
  15.4 1.8 %collective-permute-start.2 = (bf16[8,16384]{1,0:T(8,128)(2,1)S(1)}, bf16[8,16384]{1,0:T(8,128)(2,1)S(1)}, u32[]{:S(2)}, u32[]{:S(2)}) collective-permute-start(bf16[8,16384]{1,0:T(8,128)(2,1)S(1)} %pad_maximum_fusion.1), channel_id=1, source_target_pairs={{0,2},{1,3},{2,0},{3,1},{4,6},{5,7},{6,4},{7,5},{8,10},{9,11},{10,... | collective-permute-start | bytes 786440 | tf_op jit(solution)/shard_map/ppermute | solution.py:183
  17.1 4.7 %collective-permute-done.2 = bf16[8,16384]{1,0:T(8,128)(2,1)S(1)} collective-permute-done((bf16[8,16384]{1,0:T(8,128)(2,1)S(1)}, bf16[8,16384]{1,0:T(8,128)(2,1)S(1)}, u32[]{:S(2)}, u32[]{:S(2)}) %collective-permute-start.2) | collective-permute-done | bytes 262176 | tf_op jit(solution)/shard_map/ppermute | solution.py:183
  21.8 0.3 pad_maximum_fusion.mine
  22.2 0.1 collective-permute-start.3
  22.2 3.5 %shard_map.131.g_hi.g_part = bf16[4096,1024]{1,0:T(8,128)(2,1)S(1)} custom-call(bf16[8192,1024]{1,0:T(8,128)(2,1)} %w_hbm.5), custom_call_target="tpu_custom_call" | custom-call | tf_op jit(solution)/shard_map/pallas_call | solution.py:45
  25.8 3.5 %shard_map.130.g_lo.g_part = bf16[4096,1024]{1,0:T(8,128)(2,1)S(1)} custom-call(bf16[8192,1024]{1,0:T(8,128)(2,1)} %w_hbm.5), custom_call_target="tpu_custom_call" | custom-call | tf_op jit(solution)/shard_map/pallas_call | solution.py:45
  29.3 3.5 %shard_map.133.u_hi.u_part = bf16[4096,1024]{1,0:T(8,128)(2,1)S(1)} custom-call(bf16[8192,1024]{1,0:T(8,128)(2,1)} %w_hbm.7), custom_call_target="tpu_custom_call" | custom-call | tf_op jit(solution)/shard_map/pallas_call | solution.py:45
  32.8 0.0 copy-start
  32.8 0.0 copy-start.3
  32.8 0.0 copy-start.4
  32.8 0.0 copy-start.5
  32.8 3.5 %shard_map.132.u_lo.u_part = bf16[4096,1024]{1,0:T(8,128)(2,1)S(1)} custom-call(bf16[8192,1024]{1,0:T(8,128)(2,1)} %w_hbm.7), custom_call_target="tpu_custom_call" | custom-call | tf_op jit(solution)/shard_map/pallas_call | solution.py:45
  36.4 0.0 collective-permute-done.3.theirs
  36.4 0.0 copy-done
  36.4 0.0 copy-done.3
  36.4 0.0 copy-done.4
  36.4 0.0 copy-done.5
  36.4 18.2 %forward.1 = (bf16[32,16384]{1,0:T(8,128)(2,1)S(1)}, bf16[32,1024]{1,0:T(8,128)(2,1)S(1)}, bf16[32,1024]{1,0:T(8,128)(2,1)S(1)}, bf16[32,1024]{1,0:T(8,128)(2,1)S(1)}) custom-call(bf16[16,16384]{1,0:T(8,128)(2,1)S(1)} %pad_maximum_fusion.mine, bf16[16,16384]{1,0:T(8,128)(2,1)S(1)} %collective-permute-done.3.theirs, ...), custom_call_target="tpu_custom_call" | custom-call | tf_op jit(solution)/shard_map/forward/pallas_call | solution.py:195
  54.7 5.7 %shard_map.135 = (f32[16,4096]{1,0:T(8,128)S(1)}, bf16[16,4096]{1,0:T(8,128)(2,1)S(1)}) custom-call(bf16[32,1024]{1,0:T(8,128)(2,1)S(1)} %get-tuple-element.13.grad_gate, bf16[32,1024]{1,0:T(8,128)(2,1)S(1)} %get-tuple-element.14.grad_up, bf16[4096,1024]{1,0:T(8,128)(2,1)S(1)} %shard_map.131.g_hi.g_part, bf16[4096,1024]{1,0:T(8,128)(2,1)S(1)} %shard_map.133.u_hi.u_part, ...), custom_call_target="tpu_custom_call" | custom-call | tf_op jit(solution)/shard_map/pallas_call | solution.py:218
  60.4 0.0 copy-start.1
  60.4 0.0 copy-start.2
  60.4 0.6 collective-permute-start.8
  61.0 5.7 %shard_map.134 = (f32[16,4096]{1,0:T(8,128)S(1)}, bf16[16,4096]{1,0:T(8,128)(2,1)S(1)}) custom-call(bf16[32,1024]{1,0:T(8,128)(2,1)S(1)} %get-tuple-element.13.grad_gate, bf16[32,1024]{1,0:T(8,128)(2,1)S(1)} %get-tuple-element.14.grad_up, bf16[4096,1024]{1,0:T(8,128)(2,1)S(1)} %shard_map.130.g_lo.g_part, bf16[4096,1024]{1,0:T(8,128)(2,1)S(1)} %shard_map.132.u_lo.u_part, ...), custom_call_target="tpu_custom_call" | custom-call | tf_op jit(solution)/shard_map/pallas_call | solution.py:218
  66.7 0.1 collective-permute-start.4
  66.8 2.8 %moments.1 = (f32[3,4,128,128]{3,2,1,0:T(8,128)}, f32[3,4,128,128]{3,2,1,0:T(8,128)}) custom-call(bf16[32,16384]{1,0:T(8,128)(2,1)S(1)} %get-tuple-element.19.rows, bf16[32,1024]{1,0:T(8,128)(2,1)S(1)} %get-tuple-element.20.activ, bf16[32,1024]{1,0:T(8,128)(2,1)S(1)} %get-tuple-element.14.grad_up, bf16[32,1024]{1,0:T(8,128)(2,1)S(1)} %get-tuple-element.13.grad_gate, ...), custom_call_target="tpu_custom_call" | custom-call | tf_op jit(solution)/shard_map/moments/pallas_call | solution.py:239
  69.6 0.0 collective-permute-done.8
  69.7 1.9 %collective-permute-start.9 = (bf16[8,4096]{1,0:T(8,128)(2,1)S(1)}, bf16[8,4096]{1,0:T(8,128)(2,1)S(1)}, u32[]{:S(2)}, u32[]{:S(2)}) collective-permute-start(bf16[8,4096]{1,0:T(8,128)(2,1)S(1)} %slice.82), channel_id=1, source_target_pairs={{0,2},{1,3},{2,0},{3,1},{4,6},{5,7},{6,4},{7,5},{8,10},{9,11},{10,... | collective-permute-start | bytes 196616 | tf_op jit(solution)/shard_map/ppermute | solution.py:183
  71.6 0.0 collective-permute-done.4
  71.6 0.3 collective-permute-start.5
  71.9 2.3 %collective-permute-done.9 = bf16[8,4096]{1,0:T(8,128)(2,1)S(1)} collective-permute-done((bf16[8,4096]{1,0:T(8,128)(2,1)S(1)}, bf16[8,4096]{1,0:T(8,128)(2,1)S(1)}, u32[]{:S(2)}, u32[]{:S(2)}) %collective-permute-start.9) | collective-permute-done | bytes 65568 | tf_op jit(solution)/shard_map/ppermute | solution.py:183
  74.2 1.1 %collective-permute-start.10 = (bf16[4,4096]{1,0:T(4,128)(2,1)S(1)}, bf16[4,4096]{1,0:T(4,128)(2,1)S(1)}, u32[]{:S(2)}, u32[]{:S(2)}) collective-permute-start(bf16[4,4096]{1,0:T(4,128)(2,1)S(1)} %slice.84), channel_id=1, source_target_pairs={{0,4},{1,5},{2,6},{3,7},{4,0},{5,1},{6,2},{7,3},{8,12},{9,13},{10,... | collective-permute-start | bytes 98312 | tf_op jit(solution)/shard_map/ppermute | solution.py:183
  75.4 0.6 collective-permute-done.5
  76.0 0.5 collective-permute-start.6
  76.5 1.8 %collective-permute-done.10 = bf16[4,4096]{1,0:T(4,128)(2,1)S(1)} collective-permute-done((bf16[4,4096]{1,0:T(4,128)(2,1)S(1)}, bf16[4,4096]{1,0:T(4,128)(2,1)S(1)}, u32[]{:S(2)}, u32[]{:S(2)}) %collective-permute-start.10) | collective-permute-done | bytes 32800 | tf_op jit(solution)/shard_map/ppermute | solution.py:183
  78.3 4.4 %collective-permute-start.11 = (bf16[2,4096]{1,0:T(2,128)(2,1)S(1)}, bf16[2,4096]{1,0:T(2,128)(2,1)S(1)}, u32[]{:S(2)}, u32[]{:S(2)}) collective-permute-start(bf16[2,4096]{1,0:T(2,128)(2,1)S(1)} %slice.86), channel_id=1, source_target_pairs={{0,8},{1,9},{2,10},{3,11},{4,12},{5,13},{6,14},{7,15},{8,0},{9,1},... | collective-permute-start | bytes 49160 | tf_op jit(solution)/shard_map/ppermute | solution.py:183
  82.7 0.0 collective-permute-done.6
  82.7 0.6 collective-permute-start.7
  83.4 1.0 %collective-permute-done.11 = bf16[2,4096]{1,0:T(2,128)(2,1)S(1)} collective-permute-done((bf16[2,4096]{1,0:T(2,128)(2,1)S(1)}, bf16[2,4096]{1,0:T(2,128)(2,1)S(1)}, u32[]{:S(2)}, u32[]{:S(2)}) %collective-permute-start.11) | collective-permute-done | bytes 16416 | tf_op jit(solution)/shard_map/ppermute | solution.py:183
  84.4 3.0 %collective-permute-done.7 = bf16[2,4096]{1,0:T(2,128)(2,1)S(1)} collective-permute-done((bf16[2,4096]{1,0:T(2,128)(2,1)S(1)}, bf16[2,4096]{1,0:T(2,128)(2,1)S(1)}, u32[]{:S(2)}, u32[]{:S(2)}) %collective-permute-start.7) | collective-permute-done | bytes 16416 | tf_op jit(solution)/shard_map/ppermute | solution.py:183
  87.5 0.6 pad_maximum_fusion.3
  (16 shorter events, 0.3 us)
Async XLA Ops:
  2.2 7.8 %collective-permute-start = (bf16[2,16384]{1,0:T(2,128)(2,1)S(1)}, bf16[2,16384]{1,0:T(2,128)(2,1)S(1)}, u32[]{:S(2)}, u32[]{:S(2)}) collective-permute-start(bf16[2,16384]{1,0:T(2,128)(2,1)S(1)} %constant_dynamic-update-slice_fusion), channel_id=1, source_target_pairs={{0,8},{1,9},{2,10},{3,11},{4,12},{5,13},{6,14},{7,15},{8,0},{9,1},... | collective-permute-start | bytes 196616 | tf_op jit(solution)/shard_map/ppermute | solution.py:183
  10.1 5.0 %collective-permute-start.1 = (bf16[4,16384]{1,0:T(4,128)(2,1)S(1)}, bf16[4,16384]{1,0:T(4,128)(2,1)S(1)}, u32[]{:S(2)}, u32[]{:S(2)}) collective-permute-start(bf16[4,16384]{1,0:T(4,128)(2,1)S(1)} %pad_maximum_fusion.2), channel_id=1, source_target_pairs={{0,4},{1,5},{2,6},{3,7},{4,0},{5,1},{6,2},{7,3},{8,12},{9,13},{10,... | collective-permute-start | bytes 393224 | tf_op jit(solution)/shard_map/ppermute | solution.py:183
  15.4 6.4 %collective-permute-start.2 = (bf16[8,16384]{1,0:T(8,128)(2,1)S(1)}, bf16[8,16384]{1,0:T(8,128)(2,1)S(1)}, u32[]{:S(2)}, u32[]{:S(2)}) collective-permute-start(bf16[8,16384]{1,0:T(8,128)(2,1)S(1)} %pad_maximum_fusion.1), channel_id=1, source_target_pairs={{0,2},{1,3},{2,0},{3,1},{4,6},{5,7},{6,4},{7,5},{8,10},{9,11},{10,... | collective-permute-start | bytes 786440 | tf_op jit(solution)/shard_map/ppermute | solution.py:183
  22.2 14.2 %collective-permute-start.3 = (bf16[16,16384]{1,0:T(8,128)(2,1)S(1)}, bf16[16,16384]{1,0:T(8,128)(2,1)S(1)}, u32[]{:S(2)}, u32[]{:S(2)}) collective-permute-start(bf16[16,16384]{1,0:T(8,128)(2,1)S(1)} %pad_maximum_fusion.mine), channel_id=1, source_target_pairs={{0,1},{1,0},{2,3},{3,2},{4,5},{5,4},{6,7},{7,6},{8,9},{9,8},{10,11... | collective-permute-start | bytes 1572872 | tf_op jit(solution)/shard_map/ppermute | solution.py:183
  32.8 3.6 %copy-start = (bf16[3,4,128,128]{3,2,1,0:T(8,128)(2,1)S(1)}, bf16[3,4,128,128]{3,2,1,0:T(8,128)(2,1)}, u32[]{:S(2)}) copy-start(bf16[3,4,128,128]{3,2,1,0:T(8,128)(2,1)} %deltas.5) | copy-start | bytes 1179652
  32.8 3.6 %copy-start.3 = (s32[3,4]{1,0:T(4,128)S(1)}, s32[3,4]{1,0:T(4,128)}, u32[]{:S(2)}) copy-start(s32[3,4]{1,0:T(4,128)} %model.7) | copy-start | bytes 148
  32.8 3.6 %copy-start.4 = (s32[3,4]{1,0:T(4,128)S(1)}, s32[3,4]{1,0:T(4,128)}, u32[]{:S(2)}) copy-start(s32[3,4]{1,0:T(4,128)} %hidden.7) | copy-start | bytes 148
  32.8 3.6 %copy-start.5 = (s32[3,1]{0,1:T(1,128)S(1)}, s32[3,1]{0,1:T(1,128)}, u32[]{:S(2)}) copy-start(s32[3,1]{0,1:T(1,128)} %param.19) | copy-start | bytes 40
  60.4 6.4 %copy-start.1 = (f32[3,4,128,128]{3,2,1,0:T(8,128)S(1)}, f32[3,4,128,128]{3,2,1,0:T(8,128)}, u32[]{:S(2)}) copy-start(f32[3,4,128,128]{3,2,1,0:T(8,128)} %mean.1) | copy-start | bytes 2359300
  60.4 6.4 %copy-start.2 = (f32[3,4,128,128]{3,2,1,0:T(8,128)S(1)}, f32[3,4,128,128]{3,2,1,0:T(8,128)}, u32[]{:S(2)}) copy-start(f32[3,4,128,128]{3,2,1,0:T(8,128)} %square.1) | copy-start | bytes 2359300
  60.4 9.2 %collective-permute-start.8 = (bf16[16,4096]{1,0:T(8,128)(2,1)S(1)}, bf16[16,4096]{1,0:T(8,128)(2,1)S(1)}, u32[]{:S(2)}, u32[]{:S(2)}) collective-permute-start(bf16[16,4096]{1,0:T(8,128)(2,1)S(1)} %get-tuple-element.18), channel_id=1, source_target_pairs={{0,1},{1,0},{2,3},{3,2},{4,5},{5,4},{6,7},{7,6},{8,9},{9,8},{10,11... | collective-permute-start | bytes 393224 | tf_op jit(solution)/shard_map/ppermute | solution.py:183
  66.7 4.9 %collective-permute-start.4 = (bf16[16,4096]{1,0:T(8,128)(2,1)S(1)}, bf16[16,4096]{1,0:T(8,128)(2,1)S(1)}, u32[]{:S(2)}, u32[]{:S(2)}) collective-permute-start(bf16[16,4096]{1,0:T(8,128)(2,1)S(1)} %get-tuple-element.16), channel_id=1, source_target_pairs={{0,1},{1,0},{2,3},{3,2},{4,5},{5,4},{6,7},{7,6},{8,9},{9,8},{10,11... | collective-permute-start | bytes 393224 | tf_op jit(solution)/shard_map/ppermute | solution.py:183
  69.7 4.5 %collective-permute-start.9 = (bf16[8,4096]{1,0:T(8,128)(2,1)S(1)}, bf16[8,4096]{1,0:T(8,128)(2,1)S(1)}, u32[]{:S(2)}, u32[]{:S(2)}) collective-permute-start(bf16[8,4096]{1,0:T(8,128)(2,1)S(1)} %slice.82), channel_id=1, source_target_pairs={{0,2},{1,3},{2,0},{3,1},{4,6},{5,7},{6,4},{7,5},{8,10},{9,11},{10,... | collective-permute-start | bytes 196616 | tf_op jit(solution)/shard_map/ppermute | solution.py:183
  71.6 4.3 %collective-permute-start.5 = (bf16[8,4096]{1,0:T(8,128)(2,1)S(1)}, bf16[8,4096]{1,0:T(8,128)(2,1)S(1)}, u32[]{:S(2)}, u32[]{:S(2)}) collective-permute-start(bf16[8,4096]{1,0:T(8,128)(2,1)S(1)} %slice.83), channel_id=1, source_target_pairs={{0,2},{1,3},{2,0},{3,1},{4,6},{5,7},{6,4},{7,5},{8,10},{9,11},{10,... | collective-permute-start | bytes 196616 | tf_op jit(solution)/shard_map/ppermute | solution.py:183
  74.2 4.0 %collective-permute-start.10 = (bf16[4,4096]{1,0:T(4,128)(2,1)S(1)}, bf16[4,4096]{1,0:T(4,128)(2,1)S(1)}, u32[]{:S(2)}, u32[]{:S(2)}) collective-permute-start(bf16[4,4096]{1,0:T(4,128)(2,1)S(1)} %slice.84), channel_id=1, source_target_pairs={{0,4},{1,5},{2,6},{3,7},{4,0},{5,1},{6,2},{7,3},{8,12},{9,13},{10,... | collective-permute-start | bytes 98312 | tf_op jit(solution)/shard_map/ppermute | solution.py:183
  76.0 6.7 %collective-permute-start.6 = (bf16[4,4096]{1,0:T(4,128)(2,1)S(1)}, bf16[4,4096]{1,0:T(4,128)(2,1)S(1)}, u32[]{:S(2)}, u32[]{:S(2)}) collective-permute-start(bf16[4,4096]{1,0:T(4,128)(2,1)S(1)} %slice.85), channel_id=1, source_target_pairs={{0,4},{1,5},{2,6},{3,7},{4,0},{5,1},{6,2},{7,3},{8,12},{9,13},{10,... | collective-permute-start | bytes 98312 | tf_op jit(solution)/shard_map/ppermute | solution.py:183
  78.3 6.1 %collective-permute-start.11 = (bf16[2,4096]{1,0:T(2,128)(2,1)S(1)}, bf16[2,4096]{1,0:T(2,128)(2,1)S(1)}, u32[]{:S(2)}, u32[]{:S(2)}) collective-permute-start(bf16[2,4096]{1,0:T(2,128)(2,1)S(1)} %slice.86), channel_id=1, source_target_pairs={{0,8},{1,9},{2,10},{3,11},{4,12},{5,13},{6,14},{7,15},{8,0},{9,1},... | collective-permute-start | bytes 49160 | tf_op jit(solution)/shard_map/ppermute | solution.py:183
  82.7 4.7 %collective-permute-start.7 = (bf16[2,4096]{1,0:T(2,128)(2,1)S(1)}, bf16[2,4096]{1,0:T(2,128)(2,1)S(1)}, u32[]{:S(2)}, u32[]{:S(2)}) collective-permute-start(bf16[2,4096]{1,0:T(2,128)(2,1)S(1)} %slice.87), channel_id=1, source_target_pairs={{0,8},{1,9},{2,10},{3,11},{4,12},{5,13},{6,14},{7,15},{8,0},{9,1},... | collective-permute-start | bytes 49160 | tf_op jit(solution)/shard_map/ppermute | solution.py:183

commit v2 on v1

v2 whole, which is shorter than its diff:
```python
import functools

import jax
import jax.numpy as jnp
from jax import lax
from jax.experimental import pallas as pl
from jax.experimental.pallas import tpu as pltpu
from jax.sharding import PartitionSpec as P

BS = 128
MIB = 1 << 20
ROW_BY_ROW = (((1,), (1,)), ((), ()))
BY_TOKEN = (((0,), (0,)), ((), ()))
VMEM = pl.BlockSpec(memory_space=pltpu.VMEM)
SMEM = pl.BlockSpec(memory_space=pltpu.SMEM)
HBM = pl.BlockSpec(memory_space=pltpu.HBM)


def dot(a, b, dims=(((1,), (0,)), ((), ()))):
    return lax.dot_general(a, b, dims, preferred_element_type=jnp.float32)


def load_kernel(start, w_hbm, out_ref, sem):
    copy, _ = start_copies(w_hbm, start, out_ref, sem)

    def finish(i, carry):
        copy(i).wait()
        return carry

    lax.fori_loop(0, sem.shape[0], finish, 0)


def in_hbm(value):
    return pltpu.with_memory_space_constraint(value, pltpu.HBM)


def load(weight, start, rows):
    chunks = 2
    return pl.pallas_call(
        functools.partial(load_kernel, start),
        out_shape=pltpu.VMEM((rows, weight.shape[1]), weight.dtype),
        in_specs=[HBM],
        out_specs=VMEM,
        scratch_shapes=[pltpu.SemaphoreType.DMA((chunks,))],
        compiler_params=pltpu.CompilerParams(vmem_limit_bytes=MIB),
    )(in_hbm(weight))


def add_blocks(acc, source, deltas, m, model, hidden, live, transposed):
    blocks = acc.shape[1] // BS
    for s in range(deltas.shape[1]):
        at_m = pl.ds(pl.multiple_of(model[m, s] * BS, BS), BS)
        at_h = pl.ds(pl.multiple_of(lax.rem(hidden[m, s], blocks) * BS, BS), BS)
        active = jnp.where(s < live[m], deltas[m, s], jnp.zeros_like(deltas[m, s]))
        if transposed:
            acc[:, at_h] += dot(source[:, at_m], active, ROW_BY_ROW)
        else:
            acc[:, at_h] += dot(source[:, at_m], active)


def start_copies(source, start, target, sem):
    step = target.shape[0] // sem.shape[0]

    def copy(i):
        at = pl.multiple_of(i * step, step)
        return pltpu.make_async_copy(
            source.at[pl.ds(start + at, step)], target.at[pl.ds(at, step)], sem.at[i]
        )

    def begin(i, carry):
        copy(i).start()
        return carry

    lax.fori_loop(0, sem.shape[0], begin, 0)
    return copy, step


def forward_kernel(
    mine, theirs, g_lo, g_hi, u_lo, u_hi, w_down, deltas, model, hidden, live,
    x_ref, dy_ref, activ_ref, up_ref, gate_ref, gate_acc, up_acc, act_acc, d_part, sem,
):
    copy, step = start_copies(w_down, 0, d_part, sem)
    half, width = mine.shape[0], x_ref.shape[1]
    depth = g_lo.shape[0]
    x_ref[0:half, :] = mine[:, 0:width]
    x_ref[half:, :] = theirs[:, 0:width]
    dy_ref[0:half, :] = mine[:, width:]
    dy_ref[half:, :] = theirs[:, width:]
    gate_acc[...] = dot(x_ref[:, 0:depth], g_lo[...])
    gate_acc[...] += dot(x_ref[:, depth:], g_hi[...])
    up_acc[...] = dot(x_ref[:, 0:depth], u_lo[...])
    up_acc[...] += dot(x_ref[:, depth:], u_hi[...])
    add_blocks(gate_acc, x_ref, deltas, 0, model, hidden, live, False)
    add_blocks(up_acc, x_ref, deltas, 1, model, hidden, live, False)

    def down(i, carry):
        copy(i).wait()
        at = pl.ds(pl.multiple_of(i * step, step), step)
        act_acc[:, at] = dot(d_part[at, :], dy_ref[...], ROW_BY_ROW).T
        return carry

    lax.fori_loop(0, sem.shape[0], down, 0)
    add_blocks(act_acc, dy_ref, deltas, 2, model, hidden, live, True)
    gate, up, grad_act = gate_acc[...], up_acc[...], act_acc[...]
    sigma = jax.nn.sigmoid(gate)
    silu_gate = gate * sigma
    activ_ref[...] = (silu_gate * up).astype(jnp.bfloat16)
    up_ref[...] = (grad_act * silu_gate).astype(jnp.bfloat16)
    gate_ref[...] = (grad_act * up * sigma * (1.0 + gate * (1.0 - sigma))).astype(jnp.bfloat16)


def backward_kernel(
    start, grad_gate, grad_up, g_part, u_part, deltas, model, hidden, live, keep_ref, send_ref, acc
):
    slots = deltas.shape[1]
    blocks = grad_gate.shape[1] // BS
    columns = g_part.shape[0]
    half = keep_ref.shape[0]
    total = dot(g_part[...], grad_gate[...], ROW_BY_ROW)
    total += dot(u_part[...], grad_up[...], ROW_BY_ROW)
    acc[...] = total.T
    for m, grad in ((0, grad_gate), (1, grad_up)):
        for s in range(slots):
            column = model[m, s] * BS - start
            inside = (s < live[m]) & (column >= 0) & (column < columns)
            at_m = pl.ds(pl.multiple_of(jnp.clip(column, 0, columns - BS), BS), BS)
            at_h = pl.ds(pl.multiple_of(lax.rem(hidden[m, s], blocks) * BS, BS), BS)
            active = jnp.where(inside, deltas[m, s], jnp.zeros_like(deltas[m, s]))
            acc[:, at_m] += dot(grad[:, at_h], active, ROW_BY_ROW)

    keep_ref[...] = acc[0:half, :]
    send_ref[...] = acc[half:, :].astype(jnp.bfloat16)


def moments_kernel(
    x_rows, dy_rows, activ, grad_up, grad_gate, model, hidden, live, mean, square, mean_out, square_out
):
    slots = mean.shape[1]
    blocks = activ.shape[1] // BS
    for m, grad in ((0, grad_gate), (1, grad_up), (2, activ)):

        @pl.when(pl.program_id(0) == m)
        def _(m=m, grad=grad):
            for s in range(slots):
                at_h = pl.ds(pl.multiple_of(lax.rem(hidden[m, s], blocks) * BS, BS), BS)
                at_m = pl.ds(pl.multiple_of(model[m, s] * BS, BS), BS)
                if m == 2:
                    block = dot(grad[:, at_h], dy_rows[:, at_m], BY_TOKEN)
                else:
                    block = dot(x_rows[:, at_m], grad[:, at_h], BY_TOKEN)
                keep = s < live[m]
                old_mean, old_square = mean[0, s], square[0, s]
                mean_out[0, s] = jnp.where(keep, 0.9 * old_mean + 0.1 * block, old_mean)
                square_out[0, s] = jnp.where(
                    keep, 0.999 * old_square + 0.001 * block * block, old_square
                )


def stack(first, second, axis):
    zero = jnp.zeros((), first.dtype)
    after = [(0, 0, 0), (0, 0, 0)]
    before = [(0, 0, 0), (0, 0, 0)]
    after[axis] = (0, second.shape[axis], 0)
    before[axis] = (first.shape[axis], 0, 0)
    return lax.pad(first, zero, after) + lax.pad(second, zero, before)


def per_device(
    devices,
    tokens,
    out_grad,
    w_gate,
    w_up,
    w_down,
    deltas,
    model_block,
    hidden_block,
    live_count,
    prior_mean,
    prior_square,
):
    width, wide = w_gate.shape
    bits = [1 << k for k in range(devices.bit_length() - 1)]
    count = tokens.shape[0] * devices
    half = count // 2
    part = width // 2
    f32, bf16 = jnp.float32, jnp.bfloat16

    def swap(value, bit):
        return lax.ppermute(value, "tensor", [(i, i ^ bit) for i in range(devices)])

    live = live_count.reshape(-1)
    positions = (model_block, hidden_block, live)
    held = stack(tokens, out_grad, 1)
    for bit in bits[:0:-1]:
        held = stack(held, swap(held, bit), 0)
    other = swap(held, bits[0])
    g_parts = [load(w_gate, i * part, part) for i in range(2)]
    u_parts = [load(w_up, i * part, part) for i in range(2)]

    x_rows, dy_rows, activ, grad_up, grad_gate = pl.pallas_call(
        forward_kernel,
        out_shape=(
            jax.ShapeDtypeStruct((count, width), bf16),
            jax.ShapeDtypeStruct((count, width), bf16),
            jax.ShapeDtypeStruct((count, wide), bf16),
            jax.ShapeDtypeStruct((count, wide), bf16),
            jax.ShapeDtypeStruct((count, wide), bf16),
        ),
        in_specs=[VMEM] * 6 + [HBM, VMEM] + [SMEM] * 3,
        out_specs=[VMEM] * 5,
        scratch_shapes=[
            pltpu.VMEM((count, wide), f32),
            pltpu.VMEM((count, wide), f32),
            pltpu.VMEM((count, wide), f32),
            pltpu.VMEM(w_down.shape, bf16),
            pltpu.SemaphoreType.DMA((max(1, min(4, wide // BS)),)),
        ],
        compiler_params=pltpu.CompilerParams(vmem_limit_bytes=19 * MIB),
        name="forward",
    )(
        held, other, *g_parts, *u_parts, in_hbm(w_down), deltas, *positions
    )

    pieces = []
    for i in range(2):
        keep, send = pl.pallas_call(
            functools.partial(backward_kernel, i * part),
            out_shape=(
                jax.ShapeDtypeStruct((half, part), f32),
                jax.ShapeDtypeStruct((half, part), bf16),
            ),
            in_specs=[VMEM] * 5 + [SMEM] * 3,
            out_specs=[VMEM] * 2,
            scratch_shapes=[pltpu.VMEM((count, part), f32)],
            compiler_params=pltpu.CompilerParams(vmem_limit_bytes=8 * MIB),
        )(grad_gate, grad_up, g_parts[i], u_parts[i], deltas, *positions)
        pieces.append(keep + swap(send, bits[0]).astype(f32))
    left = half // 2
    keep = stack(pieces[0][:left], pieces[1][:left], 1)
    send = stack(pieces[0][left:], pieces[1][left:], 1).astype(bf16)
    for bit in bits[1:-1]:
        total = keep + swap(send, bit).astype(f32)
        left //= 2
        keep, send = total[:left], total[left:].astype(bf16)
    input_grad = (keep + swap(send, bits[-1]).astype(f32)).astype(bf16)

    slots = deltas.shape[1]
    block = pl.BlockSpec((1, slots, BS, BS), lambda m: (m, 0, 0, 0))
    mean, square = pl.pallas_call(
        moments_kernel,
        grid=(3,),
        out_shape=(
            jax.ShapeDtypeStruct(prior_mean.shape, f32),
            jax.ShapeDtypeStruct(prior_square.shape, f32),
        ),
        in_specs=[VMEM] * 5 + [SMEM] * 3 + [block] * 2,
        out_specs=[block] * 2,
        compiler_params=pltpu.CompilerParams(vmem_limit_bytes=8 * MIB),
        name="moments",
    )(x_rows, dy_rows, activ, grad_up, grad_gate, *positions, prior_mean, prior_square)
    return input_grad, mean, square


def solution(mesh):
    placed = (
        P(("groups", "tensor"), None),
        P(("groups", "tensor"), None),
        P(None, "tensor"),
        P(None, "tensor"),
        P("tensor", None),
        P("groups", "tensor", None, None),
        P("groups", "tensor"),
        P("groups", "tensor"),
        P("groups", "tensor"),
        P("groups", "tensor", None, None),
        P("groups", "tensor", None, None),
    )
    devices = mesh.shape["tensor"]
    return jax.shard_map(
        functools.partial(per_device, devices),
        mesh=mesh,
        in_specs=placed,
        out_specs=(
            P(("groups", "tensor"), None),
            P("groups", "tensor", None, None),
            P("groups", "tensor", None, None),
        ),
        check_vma=False,
    )
```

time: 88.4 us -> 77.3 us (0.87)
  Pallas kernels: 46.5 us -> 39.6 us
  starting transfers between devices: 16 us -> 13.2 us
  local copies, waits for them, and re-layouts: 1.71 us -> 0.15 us
    pallas_call x6, Pallas kernels: 35.1 us -> 28.9 us  [the longest x4 14 us: load(): pl.pallas_call(functools.partial(load_kernel, start), out_shape=pltpu.VME...]
    ppermute x12 -> x9, starting transfers between devices: 16 us -> 13.2 us  [swap(): return lax.ppermute(value, 'tensor', [(i, i ^ bit) for i in range(devices)])]
    concatenate x4 -> x0, other arithmetic: 1.35 us -> none  [the longest x3 0.7 us: per_device(): held = jnp.concatenate([held, came], axis=0)]
    add x0 -> x6, other arithmetic: none -> 1.2 us  [the longest x4 1.14 us: stack(): return lax.pad(first, zero, after) + lax.pad(second, zero, before)]
    ppermute x12 -> x9, waiting for transfers between devices: 21.5 us -> 21.3 us  [swap(): return lax.ppermute(value, 'tensor', [(i, i ^ bit) for i in range(devices)])]
  transfers between devices with their start and end apart: 12 -> 9, of which waited for: 8 -> 6; matrix products, arithmetic and copies ran while one was open for 0% -> 0% of each run, Pallas kernels for 26% -> 29%
where the time goes in v2:
time: 77.3 us; the launch traced here: 77.1 us
  Pallas kernels  39.6 us (51%)
  waiting for transfers between devices  21.3 us (28%)
  starting transfers between devices  13.2 us (17%)
  other arithmetic  1.93 us (2%)
  between operations  0.86 us (1%)
    ppermute x9, waiting for transfers between devices, swap(): return lax.ppermute(value, 'tensor', [(i, i ^ bit) for i in range(devices)])  21.3 us
    pallas_call x4, Pallas kernels, load(): pl.pallas_call(functools.partial(load_kernel, start), out_shape=pltpu.VME...  14 us
    ppermute x9, starting transfers between devices, swap(): return lax.ppermute(value, 'tensor', [(i, i ^ bit) for i in range(devices)])  13.2 us
    pallas_call x1, Pallas kernels, per_device(): pl.pallas_call(forward_kernel, out_shape=(jax.ShapeDtypeStruct((count, wi...  12.1 us
    pallas_call x2, Pallas kernels, per_device(): pl.pallas_call(functools.partial(backward_kernel, i * part), out_shape=(j...  10.8 us
    pallas_call x1, Pallas kernels, per_device(): pl.pallas_call(moments_kernel, grid=(3,), out_shape=(jax.ShapeDtypeStruct...  2.79 us
  transfers between devices with their start and end apart: 9, of which 6 were waited for; matrix products, arithmetic and copies ran while one was open for 0% of the time, Pallas kernels for 29%

profile of v2, /device:TPU:0, one launch (start us, length us, event | category | flops | bytes accessed | tf_op | source)
XLA Modules:
  0.0 77.1 jit_solution(17647519445644085193)
XLA Ops:
  0.6 0.8 %pad_add_fusion.3 = bf16[2,16384]{1,0:T(2,128)(2,1)S(1)} fusion(bf16[2,8192]{1,0:T(2,128)(2,1)} %param.12, bf16[2,8192]{1,0:T(2,128)(2,1)} %param.11), kind=kLoop, calls=%fused_computation.12 | loop fusion | flops 131072 | bytes 131072 | tf_op jit(solution)/shard_map/add | solution.py:165
  1.5 4.1 %collective-permute-start = (bf16[2,16384]{1,0:T(2,128)(2,1)S(1)}, bf16[2,16384]{1,0:T(2,128)(2,1)S(1)}, u32[]{:S(2)}, u32[]{:S(2)}) collective-permute-start(bf16[2,16384]{1,0:T(2,128)(2,1)S(1)} %pad_add_fusion.3), channel_id=1, source_target_pairs={{0,8},{1,9},{2,10},{3,11},{4,12},{5,13},{6,14},{7,15},{8,0},{9,1},... | collective-permute-start | bytes 196616 | tf_op jit(solution)/shard_map/ppermute | solution.py:190
  5.6 3.6 %collective-permute-done = bf16[2,16384]{1,0:T(2,128)(2,1)S(1)} collective-permute-done((bf16[2,16384]{1,0:T(2,128)(2,1)S(1)}, bf16[2,16384]{1,0:T(2,128)(2,1)S(1)}, u32[]{:S(2)}, u32[]{:S(2)}) %collective-permute-start) | collective-permute-done | bytes 65568 | tf_op jit(solution)/shard_map/ppermute | solution.py:190
  9.2 0.1 pad_add_fusion.2
  9.4 0.6 collective-permute-start.1
  10.0 4.4 %collective-permute-done.1 = bf16[4,16384]{1,0:T(4,128)(2,1)S(1)} collective-permute-done((bf16[4,16384]{1,0:T(4,128)(2,1)S(1)}, bf16[4,16384]{1,0:T(4,128)(2,1)S(1)}, u32[]{:S(2)}, u32[]{:S(2)}) %collective-permute-start.1) | collective-permute-done | bytes 131104 | tf_op jit(solution)/shard_map/ppermute | solution.py:190
  14.4 0.1 pad_add_fusion.1
  14.6 1.8 %collective-permute-start.2 = (bf16[8,16384]{1,0:T(8,128)(2,1)S(1)}, bf16[8,16384]{1,0:T(8,128)(2,1)S(1)}, u32[]{:S(2)}, u32[]{:S(2)}) collective-permute-start(bf16[8,16384]{1,0:T(8,128)(2,1)S(1)} %pad_add_fusion.1), channel_id=1, source_target_pairs={{0,2},{1,3},{2,0},{3,1},{4,6},{5,7},{6,4},{7,5},{8,10},{9,11},{10,... | collective-permute-start | bytes 786440 | tf_op jit(solution)/shard_map/ppermute | solution.py:190
  16.3 4.7 %collective-permute-done.2 = bf16[8,16384]{1,0:T(8,128)(2,1)S(1)} collective-permute-done((bf16[8,16384]{1,0:T(8,128)(2,1)S(1)}, bf16[8,16384]{1,0:T(8,128)(2,1)S(1)}, u32[]{:S(2)}, u32[]{:S(2)}) %collective-permute-start.2) | collective-permute-done | bytes 262176 | tf_op jit(solution)/shard_map/ppermute | solution.py:190
  21.0 0.1 collective-permute-start.3
  21.1 3.5 %shard_map.131.g_hi.g_part = bf16[4096,1024]{1,0:T(8,128)(2,1)S(1)} custom-call(bf16[8192,1024]{1,0:T(8,128)(2,1)} %w_hbm.5), custom_call_target="tpu_custom_call" | custom-call | tf_op jit(solution)/shard_map/pallas_call | solution.py:39
  24.6 3.5 %shard_map.130.g_lo.g_part = bf16[4096,1024]{1,0:T(8,128)(2,1)S(1)} custom-call(bf16[8192,1024]{1,0:T(8,128)(2,1)} %w_hbm.5), custom_call_target="tpu_custom_call" | custom-call | tf_op jit(solution)/shard_map/pallas_call | solution.py:39
  28.1 3.5 %shard_map.133.u_hi.u_part = bf16[4096,1024]{1,0:T(8,128)(2,1)S(1)} custom-call(bf16[8192,1024]{1,0:T(8,128)(2,1)} %w_hbm.7), custom_call_target="tpu_custom_call" | custom-call | tf_op jit(solution)/shard_map/pallas_call | solution.py:39
  31.6 0.0 copy-start
  31.6 0.0 copy-start.3
  31.6 0.0 copy-start.4
  31.6 0.0 copy-start.5
  31.7 3.5 %shard_map.132.u_lo.u_part = bf16[4096,1024]{1,0:T(8,128)(2,1)S(1)} custom-call(bf16[8192,1024]{1,0:T(8,128)(2,1)} %w_hbm.7), custom_call_target="tpu_custom_call" | custom-call | tf_op jit(solution)/shard_map/pallas_call | solution.py:39
  35.2 0.0 collective-permute-done.3.theirs
  35.2 0.0 copy-done
  35.2 0.0 copy-done.3
  35.2 0.0 copy-done.4
  35.2 0.0 copy-done.5
  35.2 12.1 %forward.1 = (bf16[32,8192]{1,0:T(8,128)(2,1)S(1)}, bf16[32,8192]{1,0:T(8,128)(2,1)S(1)}, bf16[32,1024]{1,0:T(8,128)(2,1)S(1)}, bf16[32,1024]{1,0:T(8,128)(2,1)S(1)}, bf16[32,1024]{1,0:T(8,128)(2,1)S(1)}) custom-call(bf16[16,16384]{1,0:T(8,128)(2,1)S(1)} %pad_add_fusion.mine, bf16[16,16384]{1,0:T(8,128)(2,1)S(1)} %collective-permute-done.3.theirs, ...), custom_call_target="tpu_custom_call" | custom-call | tf_op jit(solution)/shard_map/forward/pallas_call | solution.py:201
  47.4 5.4 %shard_map.135 = (f32[16,4096]{1,0:T(8,128)S(1)}, bf16[16,4096]{1,0:T(8,128)(2,1)S(1)}) custom-call(bf16[32,1024]{1,0:T(8,128)(2,1)S(1)} %get-tuple-element.14.grad_gate, bf16[32,1024]{1,0:T(8,128)(2,1)S(1)} %get-tuple-element.15.grad_up, bf16[4096,1024]{1,0:T(8,128)(2,1)S(1)} %shard_map.131.g_hi.g_part, bf16[4096,1024]{1,0:T(8,128)(2,1)S(1)} %shard_map.133.u_hi.u_part, ...), custom_call_target="tpu_custom_call" | custom-call | tf_op jit(solution)/shard_map/pallas_call | solution.py:227
  52.7 0.0 copy-start.1
  52.8 0.0 copy-start.2
  52.8 0.6 collective-permute-start.5
  53.4 5.4 %shard_map.134 = (f32[16,4096]{1,0:T(8,128)S(1)}, bf16[16,4096]{1,0:T(8,128)(2,1)S(1)}) custom-call(bf16[32,1024]{1,0:T(8,128)(2,1)S(1)} %get-tuple-element.14.grad_gate, bf16[32,1024]{1,0:T(8,128)(2,1)S(1)} %get-tuple-element.15.grad_up, bf16[4096,1024]{1,0:T(8,128)(2,1)S(1)} %shard_map.130.g_lo.g_part, bf16[4096,1024]{1,0:T(8,128)(2,1)S(1)} %shard_map.132.u_lo.u_part, ...), custom_call_target="tpu_custom_call" | custom-call | tf_op jit(solution)/shard_map/pallas_call | solution.py:227
  58.7 0.1 collective-permute-start.4
  58.8 0.0 collective-permute-done.5
  58.9 1.3 %collective-permute-done.4 = bf16[16,4096]{1,0:T(8,128)(2,1)S(1)} collective-permute-done((bf16[16,4096]{1,0:T(8,128)(2,1)S(1)}, bf16[16,4096]{1,0:T(8,128)(2,1)S(1)}, u32[]{:S(2)}, u32[]{:S(2)}) %collective-permute-start.4) | collective-permute-done | bytes 131104 | tf_op jit(solution)/shard_map/ppermute | solution.py:190
  60.2 1.8 %collective-permute-start.6 = (bf16[8,8192]{1,0:T(8,128)(2,1)S(1)}, bf16[8,8192]{1,0:T(8,128)(2,1)S(1)}, u32[]{:S(2)}, u32[]{:S(2)}) collective-permute-start(bf16[8,8192]{1,0:T(8,128)(2,1)S(1)} %add_convert_fusion), channel_id=1, source_target_pairs={{0,2},{1,3},{2,0},{3,1},{4,6},{5,7},{6,4},{7,5},{8,10},{9,11},{10,... | collective-permute-start | bytes 393224 | tf_op jit(solution)/shard_map/ppermute | solution.py:190
  62.0 3.8 %collective-permute-done.6 = bf16[8,8192]{1,0:T(8,128)(2,1)S(1)} collective-permute-done((bf16[8,8192]{1,0:T(8,128)(2,1)S(1)}, bf16[8,8192]{1,0:T(8,128)(2,1)S(1)}, u32[]{:S(2)}, u32[]{:S(2)}) %collective-permute-start.6) | collective-permute-done | bytes 131104 | tf_op jit(solution)/shard_map/ppermute | solution.py:190
  65.9 0.8 %collective-permute-start.7 = (bf16[4,8192]{1,0:T(4,128)(2,1)S(1)}, bf16[4,8192]{1,0:T(4,128)(2,1)S(1)}, u32[]{:S(2)}, u32[]{:S(2)}) collective-permute-start(bf16[4,8192]{1,0:T(4,128)(2,1)S(1)} %slice.48), channel_id=1, source_target_pairs={{0,4},{1,5},{2,6},{3,7},{4,0},{5,1},{6,2},{7,3},{8,12},{9,13},{10,... | collective-permute-start | bytes 196616 | tf_op jit(solution)/shard_map/ppermute | solution.py:190
  66.7 3.5 %collective-permute-done.7 = bf16[4,8192]{1,0:T(4,128)(2,1)S(1)} collective-permute-done((bf16[4,8192]{1,0:T(4,128)(2,1)S(1)}, bf16[4,8192]{1,0:T(4,128)(2,1)S(1)}, u32[]{:S(2)}, u32[]{:S(2)}) %collective-permute-start.7) | collective-permute-done | bytes 65568 | tf_op jit(solution)/shard_map/ppermute | solution.py:190
  70.3 3.3 %collective-permute-start.8 = (bf16[2,8192]{1,0:T(2,128)(2,1)S(1)}, bf16[2,8192]{1,0:T(2,128)(2,1)S(1)}, u32[]{:S(2)}, u32[]{:S(2)}) collective-permute-start(bf16[2,8192]{1,0:T(2,128)(2,1)S(1)} %slice.49), channel_id=1, source_target_pairs={{0,8},{1,9},{2,10},{3,11},{4,12},{5,13},{6,14},{7,15},{8,0},{9,1},... | collective-permute-start | bytes 98312 | tf_op jit(solution)/shard_map/ppermute | solution.py:190
  73.7 0.0 copy-done.1
  73.7 0.0 copy-done.2
  73.7 2.8 %moments.1 = (f32[3,4,128,128]{3,2,1,0:T(8,128)}, f32[3,4,128,128]{3,2,1,0:T(8,128)}) custom-call(bf16[32,8192]{1,0:T(8,128)(2,1)S(1)} %get-tuple-element.20.x_rows, bf16[32,8192]{1,0:T(8,128)(2,1)S(1)} %get-tuple-element.21.dy_rows, bf16[32,1024]{1,0:T(8,128)(2,1)S(1)} %get-tuple-element.22.activ, bf16[32,1024]{1,0:T(8,128)(2,1)S(1)} %get-tuple-element.15.grad_up, ...), custom_call_target="tpu_custom_call" | custom-call | tf_op jit(solution)/shard_map/moments/pallas_call | solution.py:250
  76.5 0.0 collective-permute-done.8
  76.5 0.7 fusion
  (10 shorter events, 0.3 us)
Async XLA Ops:
  1.5 7.8 %collective-permute-start = (bf16[2,16384]{1,0:T(2,128)(2,1)S(1)}, bf16[2,16384]{1,0:T(2,128)(2,1)S(1)}, u32[]{:S(2)}, u32[]{:S(2)}) collective-permute-start(bf16[2,16384]{1,0:T(2,128)(2,1)S(1)} %pad_add_fusion.3), channel_id=1, source_target_pairs={{0,8},{1,9},{2,10},{3,11},{4,12},{5,13},{6,14},{7,15},{8,0},{9,1},... | collective-permute-start | bytes 196616 | tf_op jit(solution)/shard_map/ppermute | solution.py:190
  9.4 5.0 %collective-permute-start.1 = (bf16[4,16384]{1,0:T(4,128)(2,1)S(1)}, bf16[4,16384]{1,0:T(4,128)(2,1)S(1)}, u32[]{:S(2)}, u32[]{:S(2)}) collective-permute-start(bf16[4,16384]{1,0:T(4,128)(2,1)S(1)} %pad_add_fusion.2), channel_id=1, source_target_pairs={{0,4},{1,5},{2,6},{3,7},{4,0},{5,1},{6,2},{7,3},{8,12},{9,13},{10,... | collective-permute-start | bytes 393224 | tf_op jit(solution)/shard_map/ppermute | solution.py:190
  14.6 6.4 %collective-permute-start.2 = (bf16[8,16384]{1,0:T(8,128)(2,1)S(1)}, bf16[8,16384]{1,0:T(8,128)(2,1)S(1)}, u32[]{:S(2)}, u32[]{:S(2)}) collective-permute-start(bf16[8,16384]{1,0:T(8,128)(2,1)S(1)} %pad_add_fusion.1), channel_id=1, source_target_pairs={{0,2},{1,3},{2,0},{3,1},{4,6},{5,7},{6,4},{7,5},{8,10},{9,11},{10,... | collective-permute-start | bytes 786440 | tf_op jit(solution)/shard_map/ppermute | solution.py:190
  21.0 14.1 %collective-permute-start.3 = (bf16[16,16384]{1,0:T(8,128)(2,1)S(1)}, bf16[16,16384]{1,0:T(8,128)(2,1)S(1)}, u32[]{:S(2)}, u32[]{:S(2)}) collective-permute-start(bf16[16,16384]{1,0:T(8,128)(2,1)S(1)} %pad_add_fusion.mine), channel_id=1, source_target_pairs={{0,1},{1,0},{2,3},{3,2},{4,5},{5,4},{6,7},{7,6},{8,9},{9,8},{10,11... | collective-permute-start | bytes 1572872 | tf_op jit(solution)/shard_map/ppermute | solution.py:190
  31.6 3.6 %copy-start = (bf16[3,4,128,128]{3,2,1,0:T(8,128)(2,1)S(1)}, bf16[3,4,128,128]{3,2,1,0:T(8,128)(2,1)}, u32[]{:S(2)}) copy-start(bf16[3,4,128,128]{3,2,1,0:T(8,128)(2,1)} %deltas.5) | copy-start | bytes 1179652
  31.6 3.6 %copy-start.3 = (s32[3,4]{1,0:T(4,128)S(1)}, s32[3,4]{1,0:T(4,128)}, u32[]{:S(2)}) copy-start(s32[3,4]{1,0:T(4,128)} %model.7) | copy-start | bytes 148
  31.6 3.6 %copy-start.4 = (s32[3,4]{1,0:T(4,128)S(1)}, s32[3,4]{1,0:T(4,128)}, u32[]{:S(2)}) copy-start(s32[3,4]{1,0:T(4,128)} %hidden.7) | copy-start | bytes 148
  31.6 3.6 %copy-start.5 = (s32[3,1]{0,1:T(1,128)S(1)}, s32[3,1]{0,1:T(1,128)}, u32[]{:S(2)}) copy-start(s32[3,1]{0,1:T(1,128)} %param.19) | copy-start | bytes 40
  52.7 20.9 %copy-start.1 = (f32[3,4,128,128]{3,2,1,0:T(8,128)S(1)}, f32[3,4,128,128]{3,2,1,0:T(8,128)}, u32[]{:S(2)}) copy-start(f32[3,4,128,128]{3,2,1,0:T(8,128)} %mean.1) | copy-start | bytes 2359300
  52.8 20.9 %copy-start.2 = (f32[3,4,128,128]{3,2,1,0:T(8,128)S(1)}, f32[3,4,128,128]{3,2,1,0:T(8,128)}, u32[]{:S(2)}) copy-start(f32[3,4,128,128]{3,2,1,0:T(8,128)} %square.1) | copy-start | bytes 2359300
  52.8 6.1 %collective-permute-start.5 = (bf16[16,4096]{1,0:T(8,128)(2,1)S(1)}, bf16[16,4096]{1,0:T(8,128)(2,1)S(1)}, u32[]{:S(2)}, u32[]{:S(2)}) collective-permute-start(bf16[16,4096]{1,0:T(8,128)(2,1)S(1)} %get-tuple-element.19), channel_id=1, source_target_pairs={{0,1},{1,0},{2,3},{3,2},{4,5},{5,4},{6,7},{7,6},{8,9},{9,8},{10,11... | collective-permute-start | bytes 393224 | tf_op jit(solution)/shard_map/ppermute | solution.py:190
  58.7 1.4 %collective-permute-start.4 = (bf16[16,4096]{1,0:T(8,128)(2,1)S(1)}, bf16[16,4096]{1,0:T(8,128)(2,1)S(1)}, u32[]{:S(2)}, u32[]{:S(2)}) collective-permute-start(bf16[16,4096]{1,0:T(8,128)(2,1)S(1)} %get-tuple-element.17), channel_id=1, source_target_pairs={{0,1},{1,0},{2,3},{3,2},{4,5},{5,4},{6,7},{7,6},{8,9},{9,8},{10,11... | collective-permute-start | bytes 393224 | tf_op jit(solution)/shard_map/ppermute | solution.py:190
  60.2 5.6 %collective-permute-start.6 = (bf16[8,8192]{1,0:T(8,128)(2,1)S(1)}, bf16[8,8192]{1,0:T(8,128)(2,1)S(1)}, u32[]{:S(2)}, u32[]{:S(2)}) collective-permute-start(bf16[8,8192]{1,0:T(8,128)(2,1)S(1)} %add_convert_fusion), channel_id=1, source_target_pairs={{0,2},{1,3},{2,0},{3,1},{4,6},{5,7},{6,4},{7,5},{8,10},{9,11},{10,... | collective-permute-start | bytes 393224 | tf_op jit(solution)/shard_map/ppermute | solution.py:190
  65.9 4.3 %collective-permute-start.7 = (bf16[4,8192]{1,0:T(4,128)(2,1)S(1)}, bf16[4,8192]{1,0:T(4,128)(2,1)S(1)}, u32[]{:S(2)}, u32[]{:S(2)}) collective-permute-start(bf16[4,8192]{1,0:T(4,128)(2,1)S(1)} %slice.48), channel_id=1, source_target_pairs={{0,4},{1,5},{2,6},{3,7},{4,0},{5,1},{6,2},{7,3},{8,12},{9,13},{10,... | collective-permute-start | bytes 196616 | tf_op jit(solution)/shard_map/ppermute | solution.py:190
  70.3 6.1 %collective-permute-start.8 = (bf16[2,8192]{1,0:T(2,128)(2,1)S(1)}, bf16[2,8192]{1,0:T(2,128)(2,1)S(1)}, u32[]{:S(2)}, u32[]{:S(2)}) collective-permute-start(bf16[2,8192]{1,0:T(2,128)(2,1)S(1)} %slice.49), channel_id=1, source_target_pairs={{0,8},{1,9},{2,10},{3,11},{4,12},{5,13},{6,14},{7,15},{8,0},{9,1},... | collective-permute-start | bytes 98312 | tf_op jit(solution)/shard_map/ppermute | solution.py:190

commit v3 on v2

--- a/solution.py
+++ b/solution.py
@@ -76,9 +76,10 @@
 
 
 def forward_kernel(
-    mine, theirs, g_lo, g_hi, u_lo, u_hi, w_down, deltas, model, hidden, live,
-    x_ref, dy_ref, activ_ref, up_ref, gate_ref, gate_acc, up_acc, act_acc, d_part, sem,
-):
+    mine, theirs, g_lo, g_hi, u_lo, w_up, w_down, deltas, model, hidden, live,
+    x_ref, dy_ref, activ_ref, up_ref, gate_ref, u_hi, gate_acc, up_acc, act_acc, d_part, u_sem, sem,
+):
+    u_copy, _ = start_copies(w_up, w_up.shape[0] - u_hi.shape[0], u_hi, u_sem)
     copy, step = start_copies(w_down, 0, d_part, sem)
     half, width = mine.shape[0], x_ref.shape[1]
     depth = g_lo.shape[0]
@@ -89,6 +90,8 @@
     gate_acc[...] = dot(x_ref[:, 0:depth], g_lo[...])
     gate_acc[...] += dot(x_ref[:, depth:], g_hi[...])
     up_acc[...] = dot(x_ref[:, 0:depth], u_lo[...])
+    for i in range(u_sem.shape[0]):
+        u_copy(i).wait()
     up_acc[...] += dot(x_ref[:, depth:], u_hi[...])
     add_blocks(gate_acc, x_ref, deltas, 0, model, hidden, live, False)
     add_blocks(up_acc, x_ref, deltas, 1, model, hidden, live, False)
@@ -116,9 +119,11 @@
     blocks = grad_gate.shape[1] // BS
     columns = g_part.shape[0]
     half = keep_ref.shape[0]
-    total = dot(g_part[...], grad_gate[...], ROW_BY_ROW)
-    total += dot(u_part[...], grad_up[...], ROW_BY_ROW)
-    acc[...] = total.T
+    tall = min(1024, columns)
+    for i in range(0, columns, tall):
+        total = dot(g_part[i : i + tall, :], grad_gate[...], ROW_BY_ROW)
+        total += dot(u_part[i : i + tall, :], grad_up[...], ROW_BY_ROW)
+        acc[:, i : i + tall] = total.T
     for m, grad in ((0, grad_gate), (1, grad_up)):
         for s in range(slots):
             column = model[m, s] * BS - start
@@ -196,9 +201,9 @@
         held = stack(held, swap(held, bit), 0)
     other = swap(held, bits[0])
     g_parts = [load(w_gate, i * part, part) for i in range(2)]
-    u_parts = [load(w_up, i * part, part) for i in range(2)]
-
-    x_rows, dy_rows, activ, grad_up, grad_gate = pl.pallas_call(
+    u_lo = load(w_up, 0, part)
+
+    x_rows, dy_rows, activ, grad_up, grad_gate, u_hi = pl.pallas_call(
         forward_kernel,
         out_shape=(
             jax.ShapeDtypeStruct((count, width), bf16),
@@ -206,22 +211,25 @@
             jax.ShapeDtypeStruct((count, wide), bf16),
             jax.ShapeDtypeStruct((count, wide), bf16),
             jax.ShapeDtypeStruct((count, wide), bf16),
+            pltpu.VMEM((part, wide), bf16),
         ),
-        in_specs=[VMEM] * 6 + [HBM, VMEM] + [SMEM] * 3,
-        out_specs=[VMEM] * 5,
+        in_specs=[VMEM] * 5 + [HBM, HBM, VMEM] + [SMEM] * 3,
+        out_specs=[VMEM] * 6,
         scratch_shapes=[
             pltpu.VMEM((count, wide), f32),
             pltpu.VMEM((count, wide), f32),
             pltpu.VMEM((count, wide), f32),
             pltpu.VMEM(w_down.shape, bf16),
+            pltpu.SemaphoreType.DMA((2,)),
             pltpu.SemaphoreType.DMA((max(1, min(4, wide // BS)),)),
         ],
         compiler_params=pltpu.CompilerParams(vmem_limit_bytes=19 * MIB),
         name="forward",
     )(
-        held, other, *g_parts, *u_parts, in_hbm(w_down), deltas, *positions
+        held, other, *g_parts, u_lo, in_hbm(w_up), in_hbm(w_down), deltas, *positions
     )
 
+    u_parts = (u_lo, u_hi)
     pieces = []
     for i in range(2):
         keep, send = pl.pallas_call(

time: 77.3 us -> 73.4 us (0.950)
  Pallas kernels: 39.6 us -> 35.7 us
    pallas_call x4 -> x3, Pallas kernels: 14 us -> 10.5 us  [load(): pl.pallas_call(functools.partial(load_kernel, start), out_shape=pltpu.VME...]
  transfers between devices with their start and end apart: 9 -> 9, of which waited for: 6 -> 6; matrix products, arithmetic and copies ran while one was open for 0% -> 0% of each run, Pallas kernels for 29% -> 25%
where the time goes in v3:
time: 73.4 us; the launch traced here: 73.2 us
  Pallas kernels  35.7 us (49%)
  waiting for transfers between devices  21.3 us (29%)
  starting transfers between devices  13.2 us (18%)
  other arithmetic  1.93 us (3%)
  between operations  0.84 us (1%)
    ppermute x9, waiting for transfers between devices, swap(): return lax.ppermute(value, 'tensor', [(i, i ^ bit) for i in range(devices)])  21.3 us
    ppermute x9, starting transfers between devices, swap(): return lax.ppermute(value, 'tensor', [(i, i ^ bit) for i in range(devices)])  13.2 us
    pallas_call x1, Pallas kernels, per_device(): pl.pallas_call(forward_kernel, out_shape=(jax.ShapeDtypeStruct((count, wi...  12 us
    pallas_call x3, Pallas kernels, load(): pl.pallas_call(functools.partial(load_kernel, start), out_shape=pltpu.VME...  10.5 us
    pallas_call x2, Pallas kernels, per_device(): pl.pallas_call(functools.partial(backward_kernel, i * part), out_shape=(j...  10.4 us
    pallas_call x1, Pallas kernels, per_device(): pl.pallas_call(moments_kernel, grid=(3,), out_shape=(jax.ShapeDtypeStruct...  2.79 us
  transfers between devices with their start and end apart: 9, of which 6 were waited for; matrix products, arithmetic and copies ran while one was open for 0% of the time, Pallas kernels for 25%

profile of v3, /device:TPU:0, one launch (start us, length us, event | category | flops | bytes accessed | tf_op | source)
XLA Modules:
  0.0 73.2 jit_solution(8892502442693770596)
XLA Ops:
  0.6 0.8 %pad_add_fusion.3 = bf16[2,16384]{1,0:T(2,128)(2,1)S(1)} fusion(bf16[2,8192]{1,0:T(2,128)(2,1)} %param.12, bf16[2,8192]{1,0:T(2,128)(2,1)} %param.11), kind=kLoop, calls=%fused_computation.12 | loop fusion | flops 131072 | bytes 131072 | tf_op jit(solution)/shard_map/add | solution.py:170
  1.5 4.1 %collective-permute-start = (bf16[2,16384]{1,0:T(2,128)(2,1)S(1)}, bf16[2,16384]{1,0:T(2,128)(2,1)S(1)}, u32[]{:S(2)}, u32[]{:S(2)}) collective-permute-start(bf16[2,16384]{1,0:T(2,128)(2,1)S(1)} %pad_add_fusion.3), channel_id=1, source_target_pairs={{0,8},{1,9},{2,10},{3,11},{4,12},{5,13},{6,14},{7,15},{8,0},{9,1},... | collective-permute-start | bytes 196616 | tf_op jit(solution)/shard_map/ppermute | solution.py:195
  5.6 3.6 %collective-permute-done = bf16[2,16384]{1,0:T(2,128)(2,1)S(1)} collective-permute-done((bf16[2,16384]{1,0:T(2,128)(2,1)S(1)}, bf16[2,16384]{1,0:T(2,128)(2,1)S(1)}, u32[]{:S(2)}, u32[]{:S(2)}) %collective-permute-start) | collective-permute-done | bytes 65568 | tf_op jit(solution)/shard_map/ppermute | solution.py:195
  9.2 0.1 pad_add_fusion.2
  9.4 0.6 collective-permute-start.1
  10.0 4.4 %collective-permute-done.1 = bf16[4,16384]{1,0:T(4,128)(2,1)S(1)} collective-permute-done((bf16[4,16384]{1,0:T(4,128)(2,1)S(1)}, bf16[4,16384]{1,0:T(4,128)(2,1)S(1)}, u32[]{:S(2)}, u32[]{:S(2)}) %collective-permute-start.1) | collective-permute-done | bytes 131104 | tf_op jit(solution)/shard_map/ppermute | solution.py:195
  14.4 0.1 pad_add_fusion.1
  14.6 1.8 %collective-permute-start.2 = (bf16[8,16384]{1,0:T(8,128)(2,1)S(1)}, bf16[8,16384]{1,0:T(8,128)(2,1)S(1)}, u32[]{:S(2)}, u32[]{:S(2)}) collective-permute-start(bf16[8,16384]{1,0:T(8,128)(2,1)S(1)} %pad_add_fusion.1), channel_id=1, source_target_pairs={{0,2},{1,3},{2,0},{3,1},{4,6},{5,7},{6,4},{7,5},{8,10},{9,11},{10,... | collective-permute-start | bytes 786440 | tf_op jit(solution)/shard_map/ppermute | solution.py:195
  16.3 4.7 %collective-permute-done.2 = bf16[8,16384]{1,0:T(8,128)(2,1)S(1)} collective-permute-done((bf16[8,16384]{1,0:T(8,128)(2,1)S(1)}, bf16[8,16384]{1,0:T(8,128)(2,1)S(1)}, u32[]{:S(2)}, u32[]{:S(2)}) %collective-permute-start.2) | collective-permute-done | bytes 262176 | tf_op jit(solution)/shard_map/ppermute | solution.py:195
  21.0 0.1 collective-permute-start.3
  21.1 3.5 %shard_map.131.g_hi.g_part = bf16[4096,1024]{1,0:T(8,128)(2,1)S(1)} custom-call(bf16[8192,1024]{1,0:T(8,128)(2,1)} %w_hbm.4), custom_call_target="tpu_custom_call" | custom-call | tf_op jit(solution)/shard_map/pallas_call | solution.py:39
  24.6 3.5 %shard_map.130.g_lo.g_part = bf16[4096,1024]{1,0:T(8,128)(2,1)S(1)} custom-call(bf16[8192,1024]{1,0:T(8,128)(2,1)} %w_hbm.4), custom_call_target="tpu_custom_call" | custom-call | tf_op jit(solution)/shard_map/pallas_call | solution.py:39
  28.1 0.0 copy-start
  28.1 0.0 copy-start.3
  28.1 0.0 copy-start.4
  28.1 0.0 copy-start.5
  28.2 3.5 %shard_map.132.u_lo.u_part = bf16[4096,1024]{1,0:T(8,128)(2,1)S(1)} custom-call(bf16[8192,1024]{1,0:T(8,128)(2,1)} %w_up.1), custom_call_target="tpu_custom_call" | custom-call | tf_op jit(solution)/shard_map/pallas_call | solution.py:39
  31.7 0.0 collective-permute-done.3.theirs
  31.7 0.0 copy-done
  31.7 0.0 copy-done.3
  31.7 0.0 copy-done.4
  31.7 0.0 copy-done.5
  31.7 12.0 %forward.1 = (bf16[32,8192]{1,0:T(8,128)(2,1)S(1)}, bf16[32,8192]{1,0:T(8,128)(2,1)S(1)}, bf16[32,1024]{1,0:T(8,128)(2,1)S(1)}, bf16[32,1024]{1,0:T(8,128)(2,1)S...) custom-call(bf16[16,16384]{1,0:T(8,128)(2,1)S(1)} %pad_add_fusion.mine, ...), custom_call_target="tpu_custom_call" | custom-call | tf_op jit(solution)/shard_map/forward/pallas_call | solution.py:206
  43.8 5.2 %shard_map.134 = (f32[16,4096]{1,0:T(8,128)S(1)}, bf16[16,4096]{1,0:T(8,128)(2,1)S(1)}) custom-call(bf16[32,1024]{1,0:T(8,128)(2,1)S(1)} %get-tuple-element.15.grad_gate, bf16[32,1024]{1,0:T(8,128)(2,1)S(1)} %get-tuple-element.16.grad_up, bf16[4096,1024]{1,0:T(8,128)(2,1)S(1)} %shard_map.131.g_hi.g_part, bf16[4096,1024]{1,0:T(8,128)(2,1)S(1)} %get-tuple-element.19.u_part, ...), custom_call_target="tpu_custom_call" | custom-call | tf_op jit(solution)/shard_map/pallas_call | solution.py:235
  49.0 0.0 copy-start.1
  49.0 0.0 copy-start.2
  49.0 0.6 collective-permute-start.5
  49.6 5.2 %shard_map.133 = (f32[16,4096]{1,0:T(8,128)S(1)}, bf16[16,4096]{1,0:T(8,128)(2,1)S(1)}) custom-call(bf16[32,1024]{1,0:T(8,128)(2,1)S(1)} %get-tuple-element.15.grad_gate, bf16[32,1024]{1,0:T(8,128)(2,1)S(1)} %get-tuple-element.16.grad_up, bf16[4096,1024]{1,0:T(8,128)(2,1)S(1)} %shard_map.130.g_lo.g_part, bf16[4096,1024]{1,0:T(8,128)(2,1)S(1)} %shard_map.132.u_lo.u_part, ...), custom_call_target="tpu_custom_call" | custom-call | tf_op jit(solution)/shard_map/pallas_call | solution.py:235
  54.8 0.1 collective-permute-start.4
  54.9 0.0 collective-permute-done.5
  55.0 1.3 %collective-permute-done.4 = bf16[16,4096]{1,0:T(8,128)(2,1)S(1)} collective-permute-done((bf16[16,4096]{1,0:T(8,128)(2,1)S(1)}, bf16[16,4096]{1,0:T(8,128)(2,1)S(1)}, u32[]{:S(2)}, u32[]{:S(2)}) %collective-permute-start.4) | collective-permute-done | bytes 131104 | tf_op jit(solution)/shard_map/ppermute | solution.py:195
  56.3 1.8 %collective-permute-start.6 = (bf16[8,8192]{1,0:T(8,128)(2,1)S(1)}, bf16[8,8192]{1,0:T(8,128)(2,1)S(1)}, u32[]{:S(2)}, u32[]{:S(2)}) collective-permute-start(bf16[8,8192]{1,0:T(8,128)(2,1)S(1)} %add_convert_fusion), channel_id=1, source_target_pairs={{0,2},{1,3},{2,0},{3,1},{4,6},{5,7},{6,4},{7,5},{8,10},{9,11},{10,... | collective-permute-start | bytes 393224 | tf_op jit(solution)/shard_map/ppermute | solution.py:195
  58.1 3.8 %collective-permute-done.6 = bf16[8,8192]{1,0:T(8,128)(2,1)S(1)} collective-permute-done((bf16[8,8192]{1,0:T(8,128)(2,1)S(1)}, bf16[8,8192]{1,0:T(8,128)(2,1)S(1)}, u32[]{:S(2)}, u32[]{:S(2)}) %collective-permute-start.6) | collective-permute-done | bytes 131104 | tf_op jit(solution)/shard_map/ppermute | solution.py:195
  62.0 0.8 %collective-permute-start.7 = (bf16[4,8192]{1,0:T(4,128)(2,1)S(1)}, bf16[4,8192]{1,0:T(4,128)(2,1)S(1)}, u32[]{:S(2)}, u32[]{:S(2)}) collective-permute-start(bf16[4,8192]{1,0:T(4,128)(2,1)S(1)} %slice.48), channel_id=1, source_target_pairs={{0,4},{1,5},{2,6},{3,7},{4,0},{5,1},{6,2},{7,3},{8,12},{9,13},{10,... | collective-permute-start | bytes 196616 | tf_op jit(solution)/shard_map/ppermute | solution.py:195
  62.8 3.5 %collective-permute-done.7 = bf16[4,8192]{1,0:T(4,128)(2,1)S(1)} collective-permute-done((bf16[4,8192]{1,0:T(4,128)(2,1)S(1)}, bf16[4,8192]{1,0:T(4,128)(2,1)S(1)}, u32[]{:S(2)}, u32[]{:S(2)}) %collective-permute-start.7) | collective-permute-done | bytes 65568 | tf_op jit(solution)/shard_map/ppermute | solution.py:195
  66.4 3.3 %collective-permute-start.8 = (bf16[2,8192]{1,0:T(2,128)(2,1)S(1)}, bf16[2,8192]{1,0:T(2,128)(2,1)S(1)}, u32[]{:S(2)}, u32[]{:S(2)}) collective-permute-start(bf16[2,8192]{1,0:T(2,128)(2,1)S(1)} %slice.49), channel_id=1, source_target_pairs={{0,8},{1,9},{2,10},{3,11},{4,12},{5,13},{6,14},{7,15},{8,0},{9,1},... | collective-permute-start | bytes 98312 | tf_op jit(solution)/shard_map/ppermute | solution.py:195
  69.8 0.0 copy-done.1
  69.8 0.0 copy-done.2
  69.8 2.8 %moments.1 = (f32[3,4,128,128]{3,2,1,0:T(8,128)}, f32[3,4,128,128]{3,2,1,0:T(8,128)}) custom-call(bf16[32,8192]{1,0:T(8,128)(2,1)S(1)} %get-tuple-element.22.x_rows, bf16[32,8192]{1,0:T(8,128)(2,1)S(1)} %get-tuple-element.23.dy_rows, bf16[32,1024]{1,0:T(8,128)(2,1)S(1)} %get-tuple-element.24.activ, bf16[32,1024]{1,0:T(8,128)(2,1)S(1)} %get-tuple-element.16.grad_up, ...), custom_call_target="tpu_custom_call" | custom-call | tf_op jit(solution)/shard_map/moments/pallas_call | solution.py:258
  72.5 0.0 collective-permute-done.8
  72.5 0.7 fusion
  (10 shorter events, 0.3 us)
Async XLA Ops:
  1.5 7.8 %collective-permute-start = (bf16[2,16384]{1,0:T(2,128)(2,1)S(1)}, bf16[2,16384]{1,0:T(2,128)(2,1)S(1)}, u32[]{:S(2)}, u32[]{:S(2)}) collective-permute-start(bf16[2,16384]{1,0:T(2,128)(2,1)S(1)} %pad_add_fusion.3), channel_id=1, source_target_pairs={{0,8},{1,9},{2,10},{3,11},{4,12},{5,13},{6,14},{7,15},{8,0},{9,1},... | collective-permute-start | bytes 196616 | tf_op jit(solution)/shard_map/ppermute | solution.py:195
  9.4 5.0 %collective-permute-start.1 = (bf16[4,16384]{1,0:T(4,128)(2,1)S(1)}, bf16[4,16384]{1,0:T(4,128)(2,1)S(1)}, u32[]{:S(2)}, u32[]{:S(2)}) collective-permute-start(bf16[4,16384]{1,0:T(4,128)(2,1)S(1)} %pad_add_fusion.2), channel_id=1, source_target_pairs={{0,4},{1,5},{2,6},{3,7},{4,0},{5,1},{6,2},{7,3},{8,12},{9,13},{10,... | collective-permute-start | bytes 393224 | tf_op jit(solution)/shard_map/ppermute | solution.py:195
  14.6 6.4 %collective-permute-start.2 = (bf16[8,16384]{1,0:T(8,128)(2,1)S(1)}, bf16[8,16384]{1,0:T(8,128)(2,1)S(1)}, u32[]{:S(2)}, u32[]{:S(2)}) collective-permute-start(bf16[8,16384]{1,0:T(8,128)(2,1)S(1)} %pad_add_fusion.1), channel_id=1, source_target_pairs={{0,2},{1,3},{2,0},{3,1},{4,6},{5,7},{6,4},{7,5},{8,10},{9,11},{10,... | collective-permute-start | bytes 786440 | tf_op jit(solution)/shard_map/ppermute | solution.py:195
  21.0 10.7 %collective-permute-start.3 = (bf16[16,16384]{1,0:T(8,128)(2,1)S(1)}, bf16[16,16384]{1,0:T(8,128)(2,1)S(1)}, u32[]{:S(2)}, u32[]{:S(2)}) collective-permute-start(bf16[16,16384]{1,0:T(8,128)(2,1)S(1)} %pad_add_fusion.mine), channel_id=1, source_target_pairs={{0,1},{1,0},{2,3},{3,2},{4,5},{5,4},{6,7},{7,6},{8,9},{9,8},{10,11... | collective-permute-start | bytes 1572872 | tf_op jit(solution)/shard_map/ppermute | solution.py:195
  28.1 3.6 %copy-start = (bf16[3,4,128,128]{3,2,1,0:T(8,128)(2,1)S(1)}, bf16[3,4,128,128]{3,2,1,0:T(8,128)(2,1)}, u32[]{:S(2)}) copy-start(bf16[3,4,128,128]{3,2,1,0:T(8,128)(2,1)} %deltas.5) | copy-start | bytes 1179652
  28.1 3.6 %copy-start.3 = (s32[3,4]{1,0:T(4,128)S(1)}, s32[3,4]{1,0:T(4,128)}, u32[]{:S(2)}) copy-start(s32[3,4]{1,0:T(4,128)} %model.7) | copy-start | bytes 148
  28.1 3.6 %copy-start.4 = (s32[3,4]{1,0:T(4,128)S(1)}, s32[3,4]{1,0:T(4,128)}, u32[]{:S(2)}) copy-start(s32[3,4]{1,0:T(4,128)} %hidden.7) | copy-start | bytes 148
  28.1 3.6 %copy-start.5 = (s32[3,1]{0,1:T(1,128)S(1)}, s32[3,1]{0,1:T(1,128)}, u32[]{:S(2)}) copy-start(s32[3,1]{0,1:T(1,128)} %param.19) | copy-start | bytes 40
  49.0 20.8 %copy-start.1 = (f32[3,4,128,128]{3,2,1,0:T(8,128)S(1)}, f32[3,4,128,128]{3,2,1,0:T(8,128)}, u32[]{:S(2)}) copy-start(f32[3,4,128,128]{3,2,1,0:T(8,128)} %mean.1) | copy-start | bytes 2359300
  49.0 20.7 %copy-start.2 = (f32[3,4,128,128]{3,2,1,0:T(8,128)S(1)}, f32[3,4,128,128]{3,2,1,0:T(8,128)}, u32[]{:S(2)}) copy-start(f32[3,4,128,128]{3,2,1,0:T(8,128)} %square.1) | copy-start | bytes 2359300
  49.0 5.9 %collective-permute-start.5 = (bf16[16,4096]{1,0:T(8,128)(2,1)S(1)}, bf16[16,4096]{1,0:T(8,128)(2,1)S(1)}, u32[]{:S(2)}, u32[]{:S(2)}) collective-permute-start(bf16[16,4096]{1,0:T(8,128)(2,1)S(1)} %get-tuple-element.21), channel_id=1, source_target_pairs={{0,1},{1,0},{2,3},{3,2},{4,5},{5,4},{6,7},{7,6},{8,9},{9,8},{10,11... | collective-permute-start | bytes 393224 | tf_op jit(solution)/shard_map/ppermute | solution.py:195
  54.8 1.4 %collective-permute-start.4 = (bf16[16,4096]{1,0:T(8,128)(2,1)S(1)}, bf16[16,4096]{1,0:T(8,128)(2,1)S(1)}, u32[]{:S(2)}, u32[]{:S(2)}) collective-permute-start(bf16[16,4096]{1,0:T(8,128)(2,1)S(1)} %get-tuple-element.18), channel_id=1, source_target_pairs={{0,1},{1,0},{2,3},{3,2},{4,5},{5,4},{6,7},{7,6},{8,9},{9,8},{10,11... | collective-permute-start | bytes 393224 | tf_op jit(solution)/shard_map/ppermute | solution.py:195
  56.3 5.6 %collective-permute-start.6 = (bf16[8,8192]{1,0:T(8,128)(2,1)S(1)}, bf16[8,8192]{1,0:T(8,128)(2,1)S(1)}, u32[]{:S(2)}, u32[]{:S(2)}) collective-permute-start(bf16[8,8192]{1,0:T(8,128)(2,1)S(1)} %add_convert_fusion), channel_id=1, source_target_pairs={{0,2},{1,3},{2,0},{3,1},{4,6},{5,7},{6,4},{7,5},{8,10},{9,11},{10,... | collective-permute-start | bytes 393224 | tf_op jit(solution)/shard_map/ppermute | solution.py:195
  62.0 4.3 %collective-permute-start.7 = (bf16[4,8192]{1,0:T(4,128)(2,1)S(1)}, bf16[4,8192]{1,0:T(4,128)(2,1)S(1)}, u32[]{:S(2)}, u32[]{:S(2)}) collective-permute-start(bf16[4,8192]{1,0:T(4,128)(2,1)S(1)} %slice.48), channel_id=1, source_target_pairs={{0,4},{1,5},{2,6},{3,7},{4,0},{5,1},{6,2},{7,3},{8,12},{9,13},{10,... | collective-permute-start | bytes 196616 | tf_op jit(solution)/shard_map/ppermute | solution.py:195
  66.4 6.1 %collective-permute-start.8 = (bf16[2,8192]{1,0:T(2,128)(2,1)S(1)}, bf16[2,8192]{1,0:T(2,128)(2,1)S(1)}, u32[]{:S(2)}, u32[]{:S(2)}) collective-permute-start(bf16[2,8192]{1,0:T(2,128)(2,1)S(1)} %slice.49), channel_id=1, source_target_pairs={{0,8},{1,9},{2,10},{3,11},{4,12},{5,13},{6,14},{7,15},{8,0},{9,1},... | collective-permute-start | bytes 98312 | tf_op jit(solution)/shard_map/ppermute | solution.py:195

commit v4 on v3

--- a/solution.py
+++ b/solution.py
@@ -196,8 +196,12 @@
 
     live = live_count.reshape(-1)
     positions = (model_block, hidden_block, live)
+    near, far = bits[:-2], bits[-2:]
+    straight = [far[1], far[0], far[0] ^ far[1]]
     held = stack(tokens, out_grad, 1)
-    for bit in bits[:0:-1]:
+    came = [swap(held, bit) for bit in straight]
+    held = stack(stack(held, came[0], 0), stack(came[1], came[2], 0), 0)
+    for bit in near[:0:-1]:
         held = stack(held, swap(held, bit), 0)
     other = swap(held, bits[0])
     g_parts = [load(w_gate, i * part, part) for i in range(2)]
@@ -247,11 +251,16 @@
     left = half // 2
     keep = stack(pieces[0][:left], pieces[1][:left], 1)
     send = stack(pieces[0][left:], pieces[1][left:], 1).astype(bf16)
-    for bit in bits[1:-1]:
+    for bit in near[1:]:
         total = keep + swap(send, bit).astype(f32)
-        left //= 2
+        left = total.shape[0] // 2
         keep, send = total[:left], total[left:].astype(bf16)
-    input_grad = (keep + swap(send, bits[-1]).astype(f32)).astype(bf16)
+    rows = tokens.shape[0]
+    input_grad = total[:rows]
+    for k, bit in enumerate(straight, 1):
+        send = total[k * rows : (k + 1) * rows].astype(bf16)
+        input_grad += swap(send, bit).astype(f32)
+    input_grad = input_grad.astype(bf16)
 
     slots = deltas.shape[1]
     block = pl.BlockSpec((1, slots, BS, BS), lambda m: (m, 0, 0, 0))

time: 73.4 us -> 70.6 us (0.962)
  waiting for transfers between devices: 21.3 us -> 17 us
  starting transfers between devices: 13.2 us -> 14.6 us
    ppermute x9 -> x11, waiting for transfers between devices: 21.3 us -> 17 us  [swap(): return lax.ppermute(value, 'tensor', [(i, i ^ bit) for i in range(devices)])]
    ppermute x9 -> x11, starting transfers between devices: 13.2 us -> 14.6 us  [swap(): return lax.ppermute(value, 'tensor', [(i, i ^ bit) for i in range(devices)])]
  transfers between devices with their start and end apart: 9 -> 11, of which waited for: 6 -> 7; matrix products, arithmetic and copies ran while one was open for 0% -> 0% of each run, Pallas kernels for 25% -> 26%
where the time goes in v4:
time: 70.6 us; the launch traced here: 70.4 us
  Pallas kernels  35.7 us (51%)
  waiting for transfers between devices  17 us (24%)
  starting transfers between devices  14.6 us (21%)
  other arithmetic  2.08 us (3%)
  between operations  0.84 us (1%)
    ppermute x11, waiting for transfers between devices, swap(): return lax.ppermute(value, 'tensor', [(i, i ^ bit) for i in range(devices)])  17 us
    ppermute x11, starting transfers between devices, swap(): return lax.ppermute(value, 'tensor', [(i, i ^ bit) for i in range(devices)])  14.6 us
    pallas_call x1, Pallas kernels, per_device(): pl.pallas_call(forward_kernel, out_shape=(jax.ShapeDtypeStruct((count, wi...  12 us
    pallas_call x3, Pallas kernels, load(): pl.pallas_call(functools.partial(load_kernel, start), out_shape=pltpu.VME...  10.5 us
    pallas_call x2, Pallas kernels, per_device(): pl.pallas_call(functools.partial(backward_kernel, i * part), out_shape=(j...  10.4 us
    pallas_call x1, Pallas kernels, per_device(): pl.pallas_call(moments_kernel, grid=(3,), out_shape=(jax.ShapeDtypeStruct...  2.79 us
  transfers between devices with their start and end apart: 11, of which 7 were waited for; matrix products, arithmetic and copies ran while one was open for 0% of the time, Pallas kernels for 26%

profile of v4, /device:TPU:0, one launch (start us, length us, event | category | flops | bytes accessed | tf_op | source)
XLA Modules:
  0.0 70.4 jit_solution(16910048870072389830)
XLA Ops:
  0.6 0.8 %pad_add_fusion.4 = bf16[2,16384]{1,0:T(2,128)(2,1)S(1)} fusion(bf16[2,8192]{1,0:T(2,128)(2,1)} %param.12, bf16[2,8192]{1,0:T(2,128)(2,1)} %param.11), kind=kLoop, calls=%fused_computation.11 | loop fusion | flops 131072 | bytes 131072 | tf_op jit(solution)/shard_map/add | solution.py:170
  1.5 4.1 %collective-permute-start = (bf16[2,16384]{1,0:T(2,128)(2,1)S(1)}, bf16[2,16384]{1,0:T(2,128)(2,1)S(1)}, u32[]{:S(2)}, u32[]{:S(2)}) collective-permute-start(bf16[2,16384]{1,0:T(2,128)(2,1)S(1)} %pad_add_fusion.4), channel_id=1, source_target_pairs={{0,8},{1,9},{2,10},{3,11},{4,12},{5,13},{6,14},{7,15},{8,0},{9,1},... | collective-permute-start | bytes 196616 | tf_op jit(solution)/shard_map/ppermute | solution.py:195
  5.6 1.3 %collective-permute-start.2 = (bf16[2,16384]{1,0:T(2,128)(2,1)S(1)}, bf16[2,16384]{1,0:T(2,128)(2,1)S(1)}, u32[]{:S(2)}, u32[]{:S(2)}) collective-permute-start(bf16[2,16384]{1,0:T(2,128)(2,1)S(1)} %pad_add_fusion.4), channel_id=1, source_target_pairs={{0,12},{1,13},{2,14},{3,15},{4,8},{5,9},{6,10},{7,11},{8,4},{9,5},... | collective-permute-start | bytes 196616 | tf_op jit(solution)/shard_map/ppermute | solution.py:195
  6.9 0.2 collective-permute-start.1
  7.2 2.1 %collective-permute-done = bf16[2,16384]{1,0:T(2,128)(2,1)S(1)} collective-permute-done((bf16[2,16384]{1,0:T(2,128)(2,1)S(1)}, bf16[2,16384]{1,0:T(2,128)(2,1)S(1)}, u32[]{:S(2)}, u32[]{:S(2)}) %collective-permute-start) | collective-permute-done | bytes 65568 | tf_op jit(solution)/shard_map/ppermute | solution.py:195
  9.3 0.1 pad_add_fusion.3
  9.5 2.3 %collective-permute-done.2 = bf16[2,16384]{1,0:T(2,128)(2,1)S(1)} collective-permute-done((bf16[2,16384]{1,0:T(2,128)(2,1)S(1)}, bf16[2,16384]{1,0:T(2,128)(2,1)S(1)}, u32[]{:S(2)}, u32[]{:S(2)}) %collective-permute-start.2) | collective-permute-done | bytes 65568 | tf_op jit(solution)/shard_map/ppermute | solution.py:195
  11.8 0.1 collective-permute-done.1
  11.9 0.1 pad_add_fusion.2
  12.1 0.1 pad_add_fusion.1
  12.2 1.6 %collective-permute-start.3 = (bf16[8,16384]{1,0:T(8,128)(2,1)S(1)}, bf16[8,16384]{1,0:T(8,128)(2,1)S(1)}, u32[]{:S(2)}, u32[]{:S(2)}) collective-permute-start(bf16[8,16384]{1,0:T(8,128)(2,1)S(1)} %pad_add_fusion.1), channel_id=1, source_target_pairs={{0,2},{1,3},{2,0},{3,1},{4,6},{5,7},{6,4},{7,5},{8,10},{9,11},{10,... | collective-permute-start | bytes 786440 | tf_op jit(solution)/shard_map/ppermute | solution.py:195
  13.8 5.1 %collective-permute-done.3 = bf16[8,16384]{1,0:T(8,128)(2,1)S(1)} collective-permute-done((bf16[8,16384]{1,0:T(8,128)(2,1)S(1)}, bf16[8,16384]{1,0:T(8,128)(2,1)S(1)}, u32[]{:S(2)}, u32[]{:S(2)}) %collective-permute-start.3) | collective-permute-done | bytes 262176 | tf_op jit(solution)/shard_map/ppermute | solution.py:195
  18.9 0.1 collective-permute-start.4
  19.0 3.5 %shard_map.131.g_hi.g_part = bf16[4096,1024]{1,0:T(8,128)(2,1)S(1)} custom-call(bf16[8192,1024]{1,0:T(8,128)(2,1)} %w_hbm.4), custom_call_target="tpu_custom_call" | custom-call | tf_op jit(solution)/shard_map/pallas_call | solution.py:39
  22.5 3.5 %shard_map.130.g_lo.g_part = bf16[4096,1024]{1,0:T(8,128)(2,1)S(1)} custom-call(bf16[8192,1024]{1,0:T(8,128)(2,1)} %w_hbm.4), custom_call_target="tpu_custom_call" | custom-call | tf_op jit(solution)/shard_map/pallas_call | solution.py:39
  26.0 0.0 copy-start
  26.0 0.0 copy-start.3
  26.0 0.0 copy-start.4
  26.0 0.0 copy-start.5
  26.0 3.5 %shard_map.132.u_lo.u_part = bf16[4096,1024]{1,0:T(8,128)(2,1)S(1)} custom-call(bf16[8192,1024]{1,0:T(8,128)(2,1)} %w_up.1), custom_call_target="tpu_custom_call" | custom-call | tf_op jit(solution)/shard_map/pallas_call | solution.py:39
  29.5 0.0 collective-permute-done.4.theirs
  29.6 0.0 copy-done
  29.6 0.0 copy-done.3
  29.6 0.0 copy-done.4
  29.6 0.0 copy-done.5
  29.6 12.0 %forward.1 = (bf16[32,8192]{1,0:T(8,128)(2,1)S(1)}, bf16[32,8192]{1,0:T(8,128)(2,1)S(1)}, bf16[32,1024]{1,0:T(8,128)(2,1)S(1)}, bf16[32,1024]{1,0:T(8,128)(2,1)S...) custom-call(bf16[16,16384]{1,0:T(8,128)(2,1)S(1)} %pad_add_fusion.mine, ...), custom_call_target="tpu_custom_call" | custom-call | tf_op jit(solution)/shard_map/forward/pallas_call | solution.py:210
  41.6 5.2 %shard_map.134 = (f32[16,4096]{1,0:T(8,128)S(1)}, bf16[16,4096]{1,0:T(8,128)(2,1)S(1)}) custom-call(bf16[32,1024]{1,0:T(8,128)(2,1)S(1)} %get-tuple-element.15.grad_gate, bf16[32,1024]{1,0:T(8,128)(2,1)S(1)} %get-tuple-element.16.grad_up, bf16[4096,1024]{1,0:T(8,128)(2,1)S(1)} %shard_map.131.g_hi.g_part, bf16[4096,1024]{1,0:T(8,128)(2,1)S(1)} %get-tuple-element.19.u_part, ...), custom_call_target="tpu_custom_call" | custom-call | tf_op jit(solution)/shard_map/pallas_call | solution.py:239
  46.8 0.0 copy-start.1
  46.9 0.0 copy-start.2
  46.9 0.6 collective-permute-start.6
  47.4 5.2 %shard_map.133 = (f32[16,4096]{1,0:T(8,128)S(1)}, bf16[16,4096]{1,0:T(8,128)(2,1)S(1)}) custom-call(bf16[32,1024]{1,0:T(8,128)(2,1)S(1)} %get-tuple-element.15.grad_gate, bf16[32,1024]{1,0:T(8,128)(2,1)S(1)} %get-tuple-element.16.grad_up, bf16[4096,1024]{1,0:T(8,128)(2,1)S(1)} %shard_map.130.g_lo.g_part, bf16[4096,1024]{1,0:T(8,128)(2,1)S(1)} %shard_map.132.u_lo.u_part, ...), custom_call_target="tpu_custom_call" | custom-call | tf_op jit(solution)/shard_map/pallas_call | solution.py:239
  52.7 0.1 collective-permute-start.5
  52.7 0.0 collective-permute-done.6
  52.8 1.3 %collective-permute-done.5 = bf16[16,4096]{1,0:T(8,128)(2,1)S(1)} collective-permute-done((bf16[16,4096]{1,0:T(8,128)(2,1)S(1)}, bf16[16,4096]{1,0:T(8,128)(2,1)S(1)}, u32[]{:S(2)}, u32[]{:S(2)}) %collective-permute-start.5) | collective-permute-done | bytes 131104 | tf_op jit(solution)/shard_map/ppermute | solution.py:195
  54.2 1.8 %collective-permute-start.7 = (bf16[8,8192]{1,0:T(8,128)(2,1)S(1)}, bf16[8,8192]{1,0:T(8,128)(2,1)S(1)}, u32[]{:S(2)}, u32[]{:S(2)}) collective-permute-start(bf16[8,8192]{1,0:T(8,128)(2,1)S(1)} %add_convert_fusion), channel_id=1, source_target_pairs={{0,2},{1,3},{2,0},{3,1},{4,6},{5,7},{6,4},{7,5},{8,10},{9,11},{10,... | collective-permute-start | bytes 393224 | tf_op jit(solution)/shard_map/ppermute | solution.py:195
  56.0 3.8 %collective-permute-done.7 = bf16[8,8192]{1,0:T(8,128)(2,1)S(1)} collective-permute-done((bf16[8,8192]{1,0:T(8,128)(2,1)S(1)}, bf16[8,8192]{1,0:T(8,128)(2,1)S(1)}, u32[]{:S(2)}, u32[]{:S(2)}) %collective-permute-start.7) | collective-permute-done | bytes 131104 | tf_op jit(solution)/shard_map/ppermute | solution.py:195
  59.8 0.1 fusion.6
  59.9 4.1 %collective-permute-start.8 = (bf16[2,8192]{1,0:T(2,128)(2,1)S(1)}, bf16[2,8192]{1,0:T(2,128)(2,1)S(1)}, u32[]{:S(2)}, u32[]{:S(2)}) collective-permute-start(bf16[2,8192]{1,0:T(2,128)(2,1)S(1)} %get-tuple-element.33), channel_id=1, source_target_pairs={{0,8},{1,9},{2,10},{3,11},{4,12},{5,13},{6,14},{7,15},{8,0},{9,1},... | collective-permute-start | bytes 98312 | tf_op jit(solution)/shard_map/ppermute | solution.py:195
  64.0 0.5 collective-permute-start.10
  64.5 0.2 collective-permute-start.9
  64.7 0.0 copy-done.1
  64.7 0.0 copy-done.2
  64.7 2.8 %moments.1 = (f32[3,4,128,128]{3,2,1,0:T(8,128)}, f32[3,4,128,128]{3,2,1,0:T(8,128)}) custom-call(bf16[32,8192]{1,0:T(8,128)(2,1)S(1)} %get-tuple-element.22.x_rows, bf16[32,8192]{1,0:T(8,128)(2,1)S(1)} %get-tuple-element.23.dy_rows, bf16[32,1024]{1,0:T(8,128)(2,1)S(1)} %get-tuple-element.24.activ, bf16[32,1024]{1,0:T(8,128)(2,1)S(1)} %get-tuple-element.16.grad_up, ...), custom_call_target="tpu_custom_call" | custom-call | tf_op jit(solution)/shard_map/moments/pallas_call | solution.py:267
  67.5 0.0 collective-permute-done.8
  67.5 2.3 %collective-permute-done.10 = bf16[2,8192]{1,0:T(2,128)(2,1)S(1)} collective-permute-done((bf16[2,8192]{1,0:T(2,128)(2,1)S(1)}, bf16[2,8192]{1,0:T(2,128)(2,1)S(1)}, u32[]{:S(2)}, u32[]{:S(2)}) %collective-permute-start.10) | collective-permute-done | bytes 32800 | tf_op jit(solution)/shard_map/ppermute | solution.py:195
  69.7 0.0 collective-permute-done.9
  69.7 0.7 fusion.2
  (7 shorter events, 0.2 us)
Async XLA Ops:
  1.5 7.8 %collective-permute-start = (bf16[2,16384]{1,0:T(2,128)(2,1)S(1)}, bf16[2,16384]{1,0:T(2,128)(2,1)S(1)}, u32[]{:S(2)}, u32[]{:S(2)}) collective-permute-start(bf16[2,16384]{1,0:T(2,128)(2,1)S(1)} %pad_add_fusion.4), channel_id=1, source_target_pairs={{0,8},{1,9},{2,10},{3,11},{4,12},{5,13},{6,14},{7,15},{8,0},{9,1},... | collective-permute-start | bytes 196616 | tf_op jit(solution)/shard_map/ppermute | solution.py:195
  5.6 6.2 %collective-permute-start.2 = (bf16[2,16384]{1,0:T(2,128)(2,1)S(1)}, bf16[2,16384]{1,0:T(2,128)(2,1)S(1)}, u32[]{:S(2)}, u32[]{:S(2)}) collective-permute-start(bf16[2,16384]{1,0:T(2,128)(2,1)S(1)} %pad_add_fusion.4), channel_id=1, source_target_pairs={{0,12},{1,13},{2,14},{3,15},{4,8},{5,9},{6,10},{7,11},{8,4},{9,5},... | collective-permute-start | bytes 196616 | tf_op jit(solution)/shard_map/ppermute | solution.py:195
  6.9 5.0 %collective-permute-start.1 = (bf16[2,16384]{1,0:T(2,128)(2,1)S(1)}, bf16[2,16384]{1,0:T(2,128)(2,1)S(1)}, u32[]{:S(2)}, u32[]{:S(2)}) collective-permute-start(bf16[2,16384]{1,0:T(2,128)(2,1)S(1)} %pad_add_fusion.4), channel_id=1, source_target_pairs={{0,4},{1,5},{2,6},{3,7},{4,0},{5,1},{6,2},{7,3},{8,12},{9,13},{10,... | collective-permute-start | bytes 196616 | tf_op jit(solution)/shard_map/ppermute | solution.py:195
  12.2 6.7 %collective-permute-start.3 = (bf16[8,16384]{1,0:T(8,128)(2,1)S(1)}, bf16[8,16384]{1,0:T(8,128)(2,1)S(1)}, u32[]{:S(2)}, u32[]{:S(2)}) collective-permute-start(bf16[8,16384]{1,0:T(8,128)(2,1)S(1)} %pad_add_fusion.1), channel_id=1, source_target_pairs={{0,2},{1,3},{2,0},{3,1},{4,6},{5,7},{6,4},{7,5},{8,10},{9,11},{10,... | collective-permute-start | bytes 786440 | tf_op jit(solution)/shard_map/ppermute | solution.py:195
  18.9 10.7 %collective-permute-start.4 = (bf16[16,16384]{1,0:T(8,128)(2,1)S(1)}, bf16[16,16384]{1,0:T(8,128)(2,1)S(1)}, u32[]{:S(2)}, u32[]{:S(2)}) collective-permute-start(bf16[16,16384]{1,0:T(8,128)(2,1)S(1)} %pad_add_fusion.mine), channel_id=1, source_target_pairs={{0,1},{1,0},{2,3},{3,2},{4,5},{5,4},{6,7},{7,6},{8,9},{9,8},{10,11... | collective-permute-start | bytes 1572872 | tf_op jit(solution)/shard_map/ppermute | solution.py:195
  26.0 3.6 %copy-start = (bf16[3,4,128,128]{3,2,1,0:T(8,128)(2,1)S(1)}, bf16[3,4,128,128]{3,2,1,0:T(8,128)(2,1)}, u32[]{:S(2)}) copy-start(bf16[3,4,128,128]{3,2,1,0:T(8,128)(2,1)} %deltas.5) | copy-start | bytes 1179652
  26.0 3.6 %copy-start.3 = (s32[3,4]{1,0:T(4,128)S(1)}, s32[3,4]{1,0:T(4,128)}, u32[]{:S(2)}) copy-start(s32[3,4]{1,0:T(4,128)} %model.7) | copy-start | bytes 148
  26.0 3.6 %copy-start.4 = (s32[3,4]{1,0:T(4,128)S(1)}, s32[3,4]{1,0:T(4,128)}, u32[]{:S(2)}) copy-start(s32[3,4]{1,0:T(4,128)} %hidden.7) | copy-start | bytes 148
  26.0 3.6 %copy-start.5 = (s32[3,1]{0,1:T(1,128)S(1)}, s32[3,1]{0,1:T(1,128)}, u32[]{:S(2)}) copy-start(s32[3,1]{0,1:T(1,128)} %param.19) | copy-start | bytes 40
  46.8 17.8 %copy-start.1 = (f32[3,4,128,128]{3,2,1,0:T(8,128)S(1)}, f32[3,4,128,128]{3,2,1,0:T(8,128)}, u32[]{:S(2)}) copy-start(f32[3,4,128,128]{3,2,1,0:T(8,128)} %mean.1) | copy-start | bytes 2359300
  46.9 17.8 %copy-start.2 = (f32[3,4,128,128]{3,2,1,0:T(8,128)S(1)}, f32[3,4,128,128]{3,2,1,0:T(8,128)}, u32[]{:S(2)}) copy-start(f32[3,4,128,128]{3,2,1,0:T(8,128)} %square.1) | copy-start | bytes 2359300
  46.9 5.9 %collective-permute-start.6 = (bf16[16,4096]{1,0:T(8,128)(2,1)S(1)}, bf16[16,4096]{1,0:T(8,128)(2,1)S(1)}, u32[]{:S(2)}, u32[]{:S(2)}) collective-permute-start(bf16[16,4096]{1,0:T(8,128)(2,1)S(1)} %get-tuple-element.21), channel_id=1, source_target_pairs={{0,1},{1,0},{2,3},{3,2},{4,5},{5,4},{6,7},{7,6},{8,9},{9,8},{10,11... | collective-permute-start | bytes 393224 | tf_op jit(solution)/shard_map/ppermute | solution.py:195
  52.7 1.4 %collective-permute-start.5 = (bf16[16,4096]{1,0:T(8,128)(2,1)S(1)}, bf16[16,4096]{1,0:T(8,128)(2,1)S(1)}, u32[]{:S(2)}, u32[]{:S(2)}) collective-permute-start(bf16[16,4096]{1,0:T(8,128)(2,1)S(1)} %get-tuple-element.18), channel_id=1, source_target_pairs={{0,1},{1,0},{2,3},{3,2},{4,5},{5,4},{6,7},{7,6},{8,9},{9,8},{10,11... | collective-permute-start | bytes 393224 | tf_op jit(solution)/shard_map/ppermute | solution.py:195
  54.2 5.6 %collective-permute-start.7 = (bf16[8,8192]{1,0:T(8,128)(2,1)S(1)}, bf16[8,8192]{1,0:T(8,128)(2,1)S(1)}, u32[]{:S(2)}, u32[]{:S(2)}) collective-permute-start(bf16[8,8192]{1,0:T(8,128)(2,1)S(1)} %add_convert_fusion), channel_id=1, source_target_pairs={{0,2},{1,3},{2,0},{3,1},{4,6},{5,7},{6,4},{7,5},{8,10},{9,11},{10,... | collective-permute-start | bytes 393224 | tf_op jit(solution)/shard_map/ppermute | solution.py:195
  59.9 7.5 %collective-permute-start.8 = (bf16[2,8192]{1,0:T(2,128)(2,1)S(1)}, bf16[2,8192]{1,0:T(2,128)(2,1)S(1)}, u32[]{:S(2)}, u32[]{:S(2)}) collective-permute-start(bf16[2,8192]{1,0:T(2,128)(2,1)S(1)} %get-tuple-element.33), channel_id=1, source_target_pairs={{0,8},{1,9},{2,10},{3,11},{4,12},{5,13},{6,14},{7,15},{8,0},{9,1},... | collective-permute-start | bytes 98312 | tf_op jit(solution)/shard_map/ppermute | solution.py:195
  64.0 5.7 %collective-permute-start.10 = (bf16[2,8192]{1,0:T(2,128)(2,1)S(1)}, bf16[2,8192]{1,0:T(2,128)(2,1)S(1)}, u32[]{:S(2)}, u32[]{:S(2)}) collective-permute-start(bf16[2,8192]{1,0:T(2,128)(2,1)S(1)} %get-tuple-element.34), channel_id=1, source_target_pairs={{0,12},{1,13},{2,14},{3,15},{4,8},{5,9},{6,10},{7,11},{8,4},{9,5},... | collective-permute-start | bytes 98312 | tf_op jit(solution)/shard_map/ppermute | solution.py:195
  64.5 5.3 %collective-permute-start.9 = (bf16[2,8192]{1,0:T(2,128)(2,1)S(1)}, bf16[2,8192]{1,0:T(2,128)(2,1)S(1)}, u32[]{:S(2)}, u32[]{:S(2)}) collective-permute-start(bf16[2,8192]{1,0:T(2,128)(2,1)S(1)} %get-tuple-element.35), channel_id=1, source_target_pairs={{0,4},{1,5},{2,6},{3,7},{4,0},{5,1},{6,2},{7,3},{8,12},{9,13},{10,... | collective-permute-start | bytes 98312 | tf_op jit(solution)/shard_map/ppermute | solution.py:195

commit v5 on v4

--- a/solution.py
+++ b/solution.py
@@ -35,7 +35,7 @@
 
 
 def load(weight, start, rows):
-    chunks = 2
+    chunks = 1
     return pl.pallas_call(
         functools.partial(load_kernel, start),
         out_shape=pltpu.VMEM((rows, weight.shape[1]), weight.dtype),
@@ -200,7 +200,7 @@
     straight = [far[1], far[0], far[0] ^ far[1]]
     held = stack(tokens, out_grad, 1)
     came = [swap(held, bit) for bit in straight]
-    held = stack(stack(held, came[0], 0), stack(came[1], came[2], 0), 0)
+    held = jnp.concatenate([held] + came, axis=0)
     for bit in near[:0:-1]:
         held = stack(held, swap(held, bit), 0)
     other = swap(held, bits[0])
@@ -225,7 +225,7 @@
             pltpu.VMEM((count, wide), f32),
             pltpu.VMEM(w_down.shape, bf16),
             pltpu.SemaphoreType.DMA((2,)),
-            pltpu.SemaphoreType.DMA((max(1, min(4, wide // BS)),)),
+            pltpu.SemaphoreType.DMA((max(1, min(2, wide // BS)),)),
         ],
         compiler_params=pltpu.CompilerParams(vmem_limit_bytes=19 * MIB),
         name="forward",

time: 70.6 us -> 68.7 us (0.973)
  starting transfers between devices: 14.6 us -> 13.4 us
    ppermute x11, starting transfers between devices: 14.6 us -> 13.4 us  [swap(): return lax.ppermute(value, 'tensor', [(i, i ^ bit) for i in range(devices)])]
  transfers between devices with their start and end apart: 11 -> 11, of which waited for: 7 -> 7; matrix products, arithmetic and copies ran while one was open for 0% -> 0% of each run, Pallas kernels for 26% -> 27%
where the time goes in v5:
time: 68.7 us; the launch traced here: 68.5 us
  Pallas kernels  35.2 us (51%)
  waiting for transfers between devices  16.9 us (25%)
  starting transfers between devices  13.4 us (20%)
  other arithmetic  1.97 us (3%)
  between operations  0.83 us (1%)
    ppermute x11, waiting for transfers between devices, swap(): return lax.ppermute(value, 'tensor', [(i, i ^ bit) for i in range(devices)])  16.9 us
    ppermute x11, starting transfers between devices, swap(): return lax.ppermute(value, 'tensor', [(i, i ^ bit) for i in range(devices)])  13.4 us
    pallas_call x1, Pallas kernels, per_device(): pl.pallas_call(forward_kernel, out_shape=(jax.ShapeDtypeStruct((count, wi...  11.8 us
    pallas_call x2, Pallas kernels, per_device(): pl.pallas_call(functools.partial(backward_kernel, i * part), out_shape=(j...  10.4 us
    pallas_call x3, Pallas kernels, load(): pl.pallas_call(functools.partial(load_kernel, start), out_shape=pltpu.VME...  10.2 us
    pallas_call x1, Pallas kernels, per_device(): pl.pallas_call(moments_kernel, grid=(3,), out_shape=(jax.ShapeDtypeStruct...  2.79 us
  transfers between devices with their start and end apart: 11, of which 7 were waited for; matrix products, arithmetic and copies ran while one was open for 0% of the time, Pallas kernels for 27%

profile of v5, /device:TPU:0, one launch (start us, length us, event | category | flops | bytes accessed | tf_op | source)
XLA Modules:
  0.0 68.5 jit_solution(9081682571234326498)
XLA Ops:
  0.6 0.8 %pad_add_fusion.1 = bf16[2,16384]{1,0:T(2,128)(2,1)S(1)} fusion(bf16[2,8192]{1,0:T(2,128)(2,1)} %param.12, bf16[2,8192]{1,0:T(2,128)(2,1)} %param.11), kind=kLoop, calls=%fused_computation.9 | loop fusion | flops 131072 | bytes 131072 | tf_op jit(solution)/shard_map/add | solution.py:170
  1.5 5.1 %collective-permute-start.2 = (bf16[2,16384]{1,0:T(2,128)(2,1)S(1)}, bf16[2,16384]{1,0:T(2,128)(2,1)S(1)}, u32[]{:S(2)}, u32[]{:S(2)}) collective-permute-start(bf16[2,16384]{1,0:T(2,128)(2,1)S(1)} %pad_add_fusion.1), channel_id=1, source_target_pairs={{0,12},{1,13},{2,14},{3,15},{4,8},{5,9},{6,10},{7,11},{8,4},{9,5},... | collective-permute-start | bytes 196616 | tf_op jit(solution)/shard_map/ppermute | solution.py:195
  6.6 0.0 collective-permute-start.1
  6.6 0.6 collective-permute-start
  7.3 2.2 %collective-permute-done.2 = bf16[2,16384]{1,0:T(2,128)(2,1)S(1)} collective-permute-done((bf16[2,16384]{1,0:T(2,128)(2,1)S(1)}, bf16[2,16384]{1,0:T(2,128)(2,1)S(1)}, u32[]{:S(2)}, u32[]{:S(2)}) %collective-permute-start.2) | collective-permute-done | bytes 65568 | tf_op jit(solution)/shard_map/ppermute | solution.py:195
  9.5 1.8 %collective-permute-done.1 = bf16[2,16384]{1,0:T(2,128)(2,1)S(1)} collective-permute-done((bf16[2,16384]{1,0:T(2,128)(2,1)S(1)}, bf16[2,16384]{1,0:T(2,128)(2,1)S(1)}, u32[]{:S(2)}, u32[]{:S(2)}) %collective-permute-start.1) | collective-permute-done | bytes 65568 | tf_op jit(solution)/shard_map/ppermute | solution.py:195
  11.3 1.0 %collective-permute-done = bf16[2,16384]{1,0:T(2,128)(2,1)S(1)} collective-permute-done((bf16[2,16384]{1,0:T(2,128)(2,1)S(1)}, bf16[2,16384]{1,0:T(2,128)(2,1)S(1)}, u32[]{:S(2)}, u32[]{:S(2)}) %collective-permute-start) | collective-permute-done | bytes 65568 | tf_op jit(solution)/shard_map/ppermute | solution.py:195
  12.2 0.3 pad_maximum_fusion
  12.6 1.6 %collective-permute-start.3 = (bf16[8,16384]{1,0:T(8,128)(2,1)S(1)}, bf16[8,16384]{1,0:T(8,128)(2,1)S(1)}, u32[]{:S(2)}, u32[]{:S(2)}) collective-permute-start(bf16[8,16384]{1,0:T(8,128)(2,1)S(1)} %pad_maximum_fusion), channel_id=1, source_target_pairs={{0,2},{1,3},{2,0},{3,1},{4,6},{5,7},{6,4},{7,5},{8,10},{9,11},{10,... | collective-permute-start | bytes 786440 | tf_op jit(solution)/shard_map/ppermute | solution.py:195
  14.1 5.4 %collective-permute-done.3 = bf16[8,16384]{1,0:T(8,128)(2,1)S(1)} collective-permute-done((bf16[8,16384]{1,0:T(8,128)(2,1)S(1)}, bf16[8,16384]{1,0:T(8,128)(2,1)S(1)}, u32[]{:S(2)}, u32[]{:S(2)}) %collective-permute-start.3) | collective-permute-done | bytes 262176 | tf_op jit(solution)/shard_map/ppermute | solution.py:195
  19.5 0.1 collective-permute-start.4
  19.6 3.4 %shard_map.131.g_hi.g_part = bf16[4096,1024]{1,0:T(8,128)(2,1)S(1)} custom-call(bf16[8192,1024]{1,0:T(8,128)(2,1)} %w_hbm.4), custom_call_target="tpu_custom_call" | custom-call | tf_op jit(solution)/shard_map/pallas_call | solution.py:39
  23.0 3.4 %shard_map.130.g_lo.g_part = bf16[4096,1024]{1,0:T(8,128)(2,1)S(1)} custom-call(bf16[8192,1024]{1,0:T(8,128)(2,1)} %w_hbm.4), custom_call_target="tpu_custom_call" | custom-call | tf_op jit(solution)/shard_map/pallas_call | solution.py:39
  26.4 0.0 copy-start
  26.4 0.0 copy-start.3
  26.4 0.0 copy-start.4
  26.4 0.0 copy-start.5
  26.4 3.4 %shard_map.132.u_lo.u_part = bf16[4096,1024]{1,0:T(8,128)(2,1)S(1)} custom-call(bf16[8192,1024]{1,0:T(8,128)(2,1)} %w_up.1), custom_call_target="tpu_custom_call" | custom-call | tf_op jit(solution)/shard_map/pallas_call | solution.py:39
  29.9 0.0 collective-permute-done.4.theirs
  29.9 0.0 copy-done
  29.9 0.0 copy-done.3
  29.9 0.0 copy-done.4
  29.9 0.0 copy-done.5
  29.9 11.8 %forward.1 = (bf16[32,8192]{1,0:T(8,128)(2,1)S(1)}, bf16[32,8192]{1,0:T(8,128)(2,1)S(1)}, bf16[32,1024]{1,0:T(8,128)(2,1)S(1)}, bf16[32,1024]{1,0:T(8,128)(2,1)S...) custom-call(bf16[16,16384]{1,0:T(8,128)(2,1)S(1)} %pad_add_fusion.mine, ...), custom_call_target="tpu_custom_call" | custom-call | tf_op jit(solution)/shard_map/forward/pallas_call | solution.py:210
  41.7 5.2 %shard_map.134 = (f32[16,4096]{1,0:T(8,128)S(1)}, bf16[16,4096]{1,0:T(8,128)(2,1)S(1)}) custom-call(bf16[32,1024]{1,0:T(8,128)(2,1)S(1)} %get-tuple-element.15.grad_gate, bf16[32,1024]{1,0:T(8,128)(2,1)S(1)} %get-tuple-element.16.grad_up, bf16[4096,1024]{1,0:T(8,128)(2,1)S(1)} %shard_map.131.g_hi.g_part, bf16[4096,1024]{1,0:T(8,128)(2,1)S(1)} %get-tuple-element.19.u_part, ...), custom_call_target="tpu_custom_call" | custom-call | tf_op jit(solution)/shard_map/pallas_call | solution.py:239
  46.9 0.0 copy-start.1
  47.0 0.0 copy-start.2
  47.0 0.6 collective-permute-start.6
  47.5 5.2 %shard_map.133 = (f32[16,4096]{1,0:T(8,128)S(1)}, bf16[16,4096]{1,0:T(8,128)(2,1)S(1)}) custom-call(bf16[32,1024]{1,0:T(8,128)(2,1)S(1)} %get-tuple-element.15.grad_gate, bf16[32,1024]{1,0:T(8,128)(2,1)S(1)} %get-tuple-element.16.grad_up, bf16[4096,1024]{1,0:T(8,128)(2,1)S(1)} %shard_map.130.g_lo.g_part, bf16[4096,1024]{1,0:T(8,128)(2,1)S(1)} %shard_map.132.u_lo.u_part, ...), custom_call_target="tpu_custom_call" | custom-call | tf_op jit(solution)/shard_map/pallas_call | solution.py:239
  52.7 0.1 collective-permute-start.5
  52.8 0.0 collective-permute-done.6
  52.9 1.3 %collective-permute-done.5 = bf16[16,4096]{1,0:T(8,128)(2,1)S(1)} collective-permute-done((bf16[16,4096]{1,0:T(8,128)(2,1)S(1)}, bf16[16,4096]{1,0:T(8,128)(2,1)S(1)}, u32[]{:S(2)}, u32[]{:S(2)}) %collective-permute-start.5) | collective-permute-done | bytes 131104 | tf_op jit(solution)/shard_map/ppermute | solution.py:195
  54.2 1.8 %collective-permute-start.7 = (bf16[8,8192]{1,0:T(8,128)(2,1)S(1)}, bf16[8,8192]{1,0:T(8,128)(2,1)S(1)}, u32[]{:S(2)}, u32[]{:S(2)}) collective-permute-start(bf16[8,8192]{1,0:T(8,128)(2,1)S(1)} %add_convert_fusion), channel_id=1, source_target_pairs={{0,2},{1,3},{2,0},{3,1},{4,6},{5,7},{6,4},{7,5},{8,10},{9,11},{10,... | collective-permute-start | bytes 393224 | tf_op jit(solution)/shard_map/ppermute | solution.py:195
  56.0 3.8 %collective-permute-done.7 = bf16[8,8192]{1,0:T(8,128)(2,1)S(1)} collective-permute-done((bf16[8,8192]{1,0:T(8,128)(2,1)S(1)}, bf16[8,8192]{1,0:T(8,128)(2,1)S(1)}, u32[]{:S(2)}, u32[]{:S(2)}) %collective-permute-start.7) | collective-permute-done | bytes 131104 | tf_op jit(solution)/shard_map/ppermute | solution.py:195
  59.9 0.1 fusion.6
  60.0 2.0 %collective-permute-start.8 = (bf16[2,8192]{1,0:T(2,128)(2,1)S(1)}, bf16[2,8192]{1,0:T(2,128)(2,1)S(1)}, u32[]{:S(2)}, u32[]{:S(2)}) collective-permute-start(bf16[2,8192]{1,0:T(2,128)(2,1)S(1)} %get-tuple-element.33), channel_id=1, source_target_pairs={{0,8},{1,9},{2,10},{3,11},{4,12},{5,13},{6,14},{7,15},{8,0},{9,1},... | collective-permute-start | bytes 98312 | tf_op jit(solution)/shard_map/ppermute | solution.py:195
  62.0 1.5 %collective-permute-start.10 = (bf16[2,8192]{1,0:T(2,128)(2,1)S(1)}, bf16[2,8192]{1,0:T(2,128)(2,1)S(1)}, u32[]{:S(2)}, u32[]{:S(2)}) collective-permute-start(bf16[2,8192]{1,0:T(2,128)(2,1)S(1)} %get-tuple-element.34), channel_id=1, source_target_pairs={{0,12},{1,13},{2,14},{3,15},{4,8},{5,9},{6,10},{7,11},{8,4},{9,5},... | collective-permute-start | bytes 98312 | tf_op jit(solution)/shard_map/ppermute | solution.py:195
  63.5 0.0 collective-permute-start.9
  63.5 0.0 copy-done.1
  63.5 0.0 copy-done.2
  63.5 2.8 %moments.1 = (f32[3,4,128,128]{3,2,1,0:T(8,128)}, f32[3,4,128,128]{3,2,1,0:T(8,128)}) custom-call(bf16[32,8192]{1,0:T(8,128)(2,1)S(1)} %get-tuple-element.22.x_rows, bf16[32,8192]{1,0:T(8,128)(2,1)S(1)} %get-tuple-element.23.dy_rows, bf16[32,1024]{1,0:T(8,128)(2,1)S(1)} %get-tuple-element.24.activ, bf16[32,1024]{1,0:T(8,128)(2,1)S(1)} %get-tuple-element.16.grad_up, ...), custom_call_target="tpu_custom_call" | custom-call | tf_op jit(solution)/shard_map/moments/pallas_call | solution.py:267
  66.3 0.0 collective-permute-done.8
  66.3 1.4 %collective-permute-done.10 = bf16[2,8192]{1,0:T(2,128)(2,1)S(1)} collective-permute-done((bf16[2,8192]{1,0:T(2,128)(2,1)S(1)}, bf16[2,8192]{1,0:T(2,128)(2,1)S(1)}, u32[]{:S(2)}, u32[]{:S(2)}) %collective-permute-start.10) | collective-permute-done | bytes 32800 | tf_op jit(solution)/shard_map/ppermute | solution.py:195
  67.8 0.0 collective-permute-done.9
  67.8 0.7 %fusion.2 = bf16[2,8192]{1,0:T(2,128)(2,1)} fusion(bf16[2,8192]{1,0:T(2,128)(2,1)S(1)} %collective-permute-done.10, bf16[2,8192]{1,0:T(2,128)(2,1)S(1)} %collective-permute-done.9, bf16[2,8192]{1,0:T(2,128)(2,1)S(1)} %collective-permute-done.8, f32[8,8192]{1,0:T(8,128)S(1)} %get-tuple-element.28), kind=kLoop, calls=%fused_computation.10 | loop fusion | flops 114688 | bytes 196608 | tf_op jit(solution)/shard_map/convert_element_type | solution.py:263
  (7 shorter events, 0.2 us)
Async XLA Ops:
  1.5 8.0 %collective-permute-start.2 = (bf16[2,16384]{1,0:T(2,128)(2,1)S(1)}, bf16[2,16384]{1,0:T(2,128)(2,1)S(1)}, u32[]{:S(2)}, u32[]{:S(2)}) collective-permute-start(bf16[2,16384]{1,0:T(2,128)(2,1)S(1)} %pad_add_fusion.1), channel_id=1, source_target_pairs={{0,12},{1,13},{2,14},{3,15},{4,8},{5,9},{6,10},{7,11},{8,4},{9,5},... | collective-permute-start | bytes 196616 | tf_op jit(solution)/shard_map/ppermute | solution.py:195
  6.6 4.7 %collective-permute-start.1 = (bf16[2,16384]{1,0:T(2,128)(2,1)S(1)}, bf16[2,16384]{1,0:T(2,128)(2,1)S(1)}, u32[]{:S(2)}, u32[]{:S(2)}) collective-permute-start(bf16[2,16384]{1,0:T(2,128)(2,1)S(1)} %pad_add_fusion.1), channel_id=1, source_target_pairs={{0,4},{1,5},{2,6},{3,7},{4,0},{5,1},{6,2},{7,3},{8,12},{9,13},{10,... | collective-permute-start | bytes 196616 | tf_op jit(solution)/shard_map/ppermute | solution.py:195
  6.6 5.6 %collective-permute-start = (bf16[2,16384]{1,0:T(2,128)(2,1)S(1)}, bf16[2,16384]{1,0:T(2,128)(2,1)S(1)}, u32[]{:S(2)}, u32[]{:S(2)}) collective-permute-start(bf16[2,16384]{1,0:T(2,128)(2,1)S(1)} %pad_add_fusion.1), channel_id=1, source_target_pairs={{0,8},{1,9},{2,10},{3,11},{4,12},{5,13},{6,14},{7,15},{8,0},{9,1},... | collective-permute-start | bytes 196616 | tf_op jit(solution)/shard_map/ppermute | solution.py:195
  12.6 6.9 %collective-permute-start.3 = (bf16[8,16384]{1,0:T(8,128)(2,1)S(1)}, bf16[8,16384]{1,0:T(8,128)(2,1)S(1)}, u32[]{:S(2)}, u32[]{:S(2)}) collective-permute-start(bf16[8,16384]{1,0:T(8,128)(2,1)S(1)} %pad_maximum_fusion), channel_id=1, source_target_pairs={{0,2},{1,3},{2,0},{3,1},{4,6},{5,7},{6,4},{7,5},{8,10},{9,11},{10,... | collective-permute-start | bytes 786440 | tf_op jit(solution)/shard_map/ppermute | solution.py:195
  19.5 10.4 %collective-permute-start.4 = (bf16[16,16384]{1,0:T(8,128)(2,1)S(1)}, bf16[16,16384]{1,0:T(8,128)(2,1)S(1)}, u32[]{:S(2)}, u32[]{:S(2)}) collective-permute-start(bf16[16,16384]{1,0:T(8,128)(2,1)S(1)} %pad_add_fusion.mine), channel_id=1, source_target_pairs={{0,1},{1,0},{2,3},{3,2},{4,5},{5,4},{6,7},{7,6},{8,9},{9,8},{10,11... | collective-permute-start | bytes 1572872 | tf_op jit(solution)/shard_map/ppermute | solution.py:195
  26.4 3.5 %copy-start = (bf16[3,4,128,128]{3,2,1,0:T(8,128)(2,1)S(1)}, bf16[3,4,128,128]{3,2,1,0:T(8,128)(2,1)}, u32[]{:S(2)}) copy-start(bf16[3,4,128,128]{3,2,1,0:T(8,128)(2,1)} %deltas.5) | copy-start | bytes 1179652
  26.4 3.5 %copy-start.3 = (s32[3,4]{1,0:T(4,128)S(1)}, s32[3,4]{1,0:T(4,128)}, u32[]{:S(2)}) copy-start(s32[3,4]{1,0:T(4,128)} %model.7) | copy-start | bytes 148
  26.4 3.5 %copy-start.4 = (s32[3,4]{1,0:T(4,128)S(1)}, s32[3,4]{1,0:T(4,128)}, u32[]{:S(2)}) copy-start(s32[3,4]{1,0:T(4,128)} %hidden.7) | copy-start | bytes 148
  26.4 3.5 %copy-start.5 = (s32[3,1]{0,1:T(1,128)S(1)}, s32[3,1]{0,1:T(1,128)}, u32[]{:S(2)}) copy-start(s32[3,1]{0,1:T(1,128)} %param.19) | copy-start | bytes 40
  46.9 16.6 %copy-start.1 = (f32[3,4,128,128]{3,2,1,0:T(8,128)S(1)}, f32[3,4,128,128]{3,2,1,0:T(8,128)}, u32[]{:S(2)}) copy-start(f32[3,4,128,128]{3,2,1,0:T(8,128)} %mean.1) | copy-start | bytes 2359300
  47.0 16.6 %copy-start.2 = (f32[3,4,128,128]{3,2,1,0:T(8,128)S(1)}, f32[3,4,128,128]{3,2,1,0:T(8,128)}, u32[]{:S(2)}) copy-start(f32[3,4,128,128]{3,2,1,0:T(8,128)} %square.1) | copy-start | bytes 2359300
  47.0 5.9 %collective-permute-start.6 = (bf16[16,4096]{1,0:T(8,128)(2,1)S(1)}, bf16[16,4096]{1,0:T(8,128)(2,1)S(1)}, u32[]{:S(2)}, u32[]{:S(2)}) collective-permute-start(bf16[16,4096]{1,0:T(8,128)(2,1)S(1)} %get-tuple-element.21), channel_id=1, source_target_pairs={{0,1},{1,0},{2,3},{3,2},{4,5},{5,4},{6,7},{7,6},{8,9},{9,8},{10,11... | collective-permute-start | bytes 393224 | tf_op jit(solution)/shard_map/ppermute | solution.py:195
  52.7 1.4 %collective-permute-start.5 = (bf16[16,4096]{1,0:T(8,128)(2,1)S(1)}, bf16[16,4096]{1,0:T(8,128)(2,1)S(1)}, u32[]{:S(2)}, u32[]{:S(2)}) collective-permute-start(bf16[16,4096]{1,0:T(8,128)(2,1)S(1)} %get-tuple-element.18), channel_id=1, source_target_pairs={{0,1},{1,0},{2,3},{3,2},{4,5},{5,4},{6,7},{7,6},{8,9},{9,8},{10,11... | collective-permute-start | bytes 393224 | tf_op jit(solution)/shard_map/ppermute | solution.py:195
  54.2 5.6 %collective-permute-start.7 = (bf16[8,8192]{1,0:T(8,128)(2,1)S(1)}, bf16[8,8192]{1,0:T(8,128)(2,1)S(1)}, u32[]{:S(2)}, u32[]{:S(2)}) collective-permute-start(bf16[8,8192]{1,0:T(8,128)(2,1)S(1)} %add_convert_fusion), channel_id=1, source_target_pairs={{0,2},{1,3},{2,0},{3,1},{4,6},{5,7},{6,4},{7,5},{8,10},{9,11},{10,... | collective-permute-start | bytes 393224 | tf_op jit(solution)/shard_map/ppermute | solution.py:195
  60.0 6.3 %collective-permute-start.8 = (bf16[2,8192]{1,0:T(2,128)(2,1)S(1)}, bf16[2,8192]{1,0:T(2,128)(2,1)S(1)}, u32[]{:S(2)}, u32[]{:S(2)}) collective-permute-start(bf16[2,8192]{1,0:T(2,128)(2,1)S(1)} %get-tuple-element.33), channel_id=1, source_target_pairs={{0,8},{1,9},{2,10},{3,11},{4,12},{5,13},{6,14},{7,15},{8,0},{9,1},... | collective-permute-start | bytes 98312 | tf_op jit(solution)/shard_map/ppermute | solution.py:195
  62.0 5.7 %collective-permute-start.10 = (bf16[2,8192]{1,0:T(2,128)(2,1)S(1)}, bf16[2,8192]{1,0:T(2,128)(2,1)S(1)}, u32[]{:S(2)}, u32[]{:S(2)}) collective-permute-start(bf16[2,8192]{1,0:T(2,128)(2,1)S(1)} %get-tuple-element.34), channel_id=1, source_target_pairs={{0,12},{1,13},{2,14},{3,15},{4,8},{5,9},{6,10},{7,11},{8,4},{9,5},... | collective-permute-start | bytes 98312 | tf_op jit(solution)/shard_map/ppermute | solution.py:195
  63.5 4.3 %collective-permute-start.9 = (bf16[2,8192]{1,0:T(2,128)(2,1)S(1)}, bf16[2,8192]{1,0:T(2,128)(2,1)S(1)}, u32[]{:S(2)}, u32[]{:S(2)}) collective-permute-start(bf16[2,8192]{1,0:T(2,128)(2,1)S(1)} %get-tuple-element.35), channel_id=1, source_target_pairs={{0,4},{1,5},{2,6},{3,7},{4,0},{5,1},{6,2},{7,3},{8,12},{9,13},{10,... | collective-permute-start | bytes 98312 | tf_op jit(solution)/shard_map/ppermute | solution.py:195
